TPU v7x, 512 devices: a whole 4x8x8 slice. The times are simulated.
512 devices in a mesh: front: 4 (over x), row: 8 (over y), col: 16 (over z, core).
Axes of the slice: x: 4, y: 8, z: 8, core: 2. Of those that a mesh axis runs over, the one named last changes fastest.
Arguments:
- contrib: float32 [32768, 4096], P(('front', 'row'), 'col'), parts along dimension 0, as said below
- front_diag: float32 [32768], P(('front', 'row')), parts along dimension 0, may hold values from 1 to 4
- child_map: int32 [8, 32], P('front'), parts along dimension 0, may hold values from 0 to 63, as said below
- pivots: int32 [16], P('front'), parts along dimension 0, may hold values from 0 to 63, as said below
Outputs:
- lfactor: float32 [32768, 512], P(('front', 'row'), 'col'), parts along dimension 0
- schur_block: float32 [32768, 8192], P(('front', 'row'), 'col'), parts along dimension 0
There are 4 independent parts, one for each index of `front`. A program takes and returns all parts, laid end to end along the dimension named above; each array names one. Nothing has to cross between parts.
Inputs may be any that keep to these rules, and one draw needn't show every extreme that they name: child_map[c, b] is b or b + 32, chosen for each child and block. `pivots`: 4 distinct front blocks. `contrib`: each child's contribution block is symmetric positive definite.
All inputs are finite; a program needn't handle non-finite values.
Results may differ from a plain program's by a relative error of at most 0.0001.
Values sent between devices are 32-bit elements; how exact they have to be, the bound alone decides.
A program may use at most 64 MiB of HBM per device.

v0:
```python
import jax
import jax.numpy as jnp
from jax import lax
from jax.sharding import PartitionSpec as P

NF = 8192
NPAN = 2
BLK = 128


highest = lax.Precision.HIGHEST


def swapped(shard, axis, bit):
    return lax.ppermute(shard, axis, [(i, i ^ 1 << bit) for i in range(lax.axis_size(axis))])


def broadcast(shard, axis, root):
    mine = lax.axis_index(axis) == root
    return lax.psum(jnp.where(mine, shard, jnp.zeros_like(shard)), axis)


def select_rows(mapping, chosen_ids, within, half_rows, row_index, row_count, row_slots):
    by_device = mapping.reshape(mapping.shape[0] // half_rows, half_rows)
    targets = jnp.take(lax.dynamic_index_in_dim(by_device, within, 1, keepdims=False), chosen_ids)
    slot_ids = jnp.arange(row_slots) * row_count + row_index
    return (targets[None, :] == slot_ids[:, None]).astype(jnp.float32)


def select_cols(mapping, col_index, col_count, col_slots):
    by_device = mapping.reshape(mapping.shape[0] // col_count, col_count)
    targets = lax.dynamic_index_in_dim(by_device, col_index, 1, keepdims=False)
    slot_ids = jnp.arange(col_slots) * col_count + col_index
    return (targets[None, :] == slot_ids[:, None]).astype(jnp.float32)


def place_blocks(pieces, row_select, col_select):
    blocks = pieces.reshape(row_select.shape[1], BLK, col_select.shape[1], BLK)
    placed = jnp.einsum("kj,jaib->kaib", row_select, blocks, precision=highest)
    placed = jnp.einsum("li,kaib->kalb", col_select, placed, precision=highest)
    return placed.reshape(row_select.shape[0] * BLK, col_select.shape[0] * BLK)


def per_device(contrib, front_diag, child_map, pivots):
    row_count = lax.axis_size("row")
    col_count = lax.axis_size("col")
    row_index = lax.axis_index("row")
    col_index = lax.axis_index("col")
    half_rows = row_count // 2
    half_bit = half_rows.bit_length() - 1
    sibling = row_index // half_rows
    within = row_index % half_rows
    local_rows = front_diag.shape[0]
    row_slots = local_rows // BLK
    col_width = NF // col_count
    col_slots = col_width // BLK
    child_rows = contrib.shape[0] // BLK
    own_map = lax.dynamic_index_in_dim(child_map, sibling, 0, keepdims=False)
    other_map = lax.dynamic_index_in_dim(child_map, 1 - sibling, 0, keepdims=False)
    partner = swapped(contrib, "row", half_bit)
    other_ids = jnp.arange(child_rows)
    own_rows = select_rows(
        own_map, jnp.arange(child_rows), within, half_rows, row_index, row_count, row_slots
    )
    other_rows = select_rows(
        other_map, other_ids, within, half_rows, row_index, row_count, row_slots
    )
    own_cols = select_cols(own_map, col_index, col_count, col_slots)
    other_cols = select_cols(other_map, col_index, col_count, col_slots)
    assembled = place_blocks(contrib, own_rows, own_cols) + place_blocks(
        partner, other_rows, other_cols
    )
    row_ids = jnp.arange(row_slots) * row_count + row_index
    col_ids = jnp.arange(col_slots) * col_count + col_index
    on_diagonal = (row_ids[:, None] == col_ids[None, :]).astype(jnp.float32)
    identity = jnp.eye(BLK, dtype=jnp.float32)
    diag_blocks = front_diag.reshape(row_slots, BLK)
    diag_part = (
        on_diagonal[:, None, :, None] * diag_blocks[:, :, None, None] * identity[None, :, None, :]
    )
    front_tile = assembled + diag_part.reshape(local_rows, col_width)
    factors = []
    for panel_index in range(NPAN):
        chosen = [pivots[2 * panel_index], pivots[2 * panel_index + 1]]
        columns = []
        for block_id in chosen:
            block_piece = lax.dynamic_slice_in_dim(front_tile, block_id // col_count * BLK, BLK, 1)
            columns.append(broadcast(block_piece, "col", block_id % col_count))
        panel_cols = jnp.concatenate(columns, axis=1)
        owned_rows = []
        for block_id in chosen:
            rows_here = lax.dynamic_slice_in_dim(panel_cols, block_id // row_count * BLK, BLK, 0)
            owned_rows.append(jnp.where(block_id % row_count == row_index, rows_here, 0.0))
        pivot_block = lax.psum(jnp.concatenate(owned_rows, axis=0), "row")
        lower_factor = jnp.linalg.cholesky(pivot_block)
        factor = lax.linalg.triangular_solve(
            lower_factor, panel_cols, left_side=False, lower=True, transpose_a=True
        )
        source_rows = []
        for slot_index in range(col_slots):
            source_rows.append(
                lax.dynamic_slice_in_dim(factor, col_ids[slot_index] // row_count * BLK, BLK, 0)
            )
        across = broadcast(jnp.concatenate(source_rows, axis=0), "row", col_index % row_count)
        update = jnp.einsum("ak,bk->ab", factor, across, precision=highest)
        row_hit = jnp.logical_or(row_ids == chosen[0], row_ids == chosen[1])
        col_hit = jnp.logical_or(col_ids == chosen[0], col_ids == chosen[1])
        row_keep = jnp.repeat(jnp.where(row_hit, 0.0, 1.0), BLK)
        col_keep = jnp.repeat(jnp.where(col_hit, 0.0, 1.0), BLK)
        front_tile = (front_tile - update) * row_keep[:, None] * col_keep[None, :]
        factors.append(factor)
    stacked = jnp.concatenate(factors, axis=1)
    col_share = stacked.shape[1] // col_count
    lfactor = lax.dynamic_slice_in_dim(stacked, col_index * col_share, col_share, 1)
    return (lfactor, front_tile)


def solution(mesh):
    placed = (P(("front", "row"), "col"), P(("front", "row")), P("front", None), P("front"))
    return jax.shard_map(
        per_device,
        mesh=mesh,
        in_specs=placed,
        out_specs=(P(("front", "row"), "col"), P(("front", "row"), "col")),
        check_vma=False,
    )
```

profile of v0, /device:TPU:6, one launch (start us, length us, event | category | flops | bytes accessed | tf_op | source)
XLA Modules:
  0.0 781.0 jit_solution(6074221105859730015)
XLA Ops:
  7.2 7.7 collective-permute-start
  15.0 0.8 fusion.55
  17.5 1.4 fusion.61
  19.0 1.7 reshape.126
  25.9 1.0 broadcast_multiply_fusion
  26.9 1.2 fusion.5
  28.0 2.3 fusion.3
  30.4 30.0 %collective-permute-done = f32[1024,256]{1,0:T(8,128)} collective-permute-done((f32[1024,256]{1,0:T(8,128)}, f32[1024,256]{1,0:T(8,128)}, u32[]{:S(2)}, u32[]{:S(2)}) %collective-permute-start) | collective-permute-done | bytes 1048608 | tf_op jit(solution)/shard_map/ppermute | solution.py:15
  60.4 1.7 reshape.129
  62.1 1.2 fusion.1
  63.3 3.7 bitcast_add_fusion
  67.0 1.5 copy.39
  68.5 1.9 copy.28
  70.4 1.2 dynamic-slice_select_fusion.2
  71.7 123.2 %all-reduce.20.cloned.1.call-done = (f32[1024,128]{0,1:T(8,128)}, f32[1024,128]{0,1:T(8,128)}) async-done(((f32[1024,128]{0,1:T(8,128)}, f32[1024,128]{0,1:T(8,128)}), (f32[1024,128]{0,1:T(8,128)}, f32[1024,128]{0,1:T(8,128)})) %all-reduce.20.cloned.1.call-update) | async-done | bytes 1048592 | tf_op jit(solution)/shard_map/psum | solution.py:20
  194.9 1.1 constant_dynamic-update-slice_fusion.3
  196.0 1.1 constant_dynamic-update-slice_fusion.2
  197.2 0.7 pad_maximum_fusion.4
  198.1 0.7 fusion.62
  213.7 1.2 or_select_fusion.2
  214.9 60.4 %all-reduce.10.cloned.1.call-done = f32[256,256]{0,1:T(8,128)} async-done(((f32[256,256]{0,1:T(8,128)}), f32[256,256]{0,1:T(8,128)}) %all-reduce.10.cloned.1.call-update) | async-done | bytes 262160 | tf_op jit(solution)/shard_map/psum | solution.py:94
  275.3 1.1 copy.13
  276.4 1.0 fusion.8
  277.4 11.7 %cholesky.130 = f32[128,128]{1,0:T(8,128)S(1)} custom-call(f32[128,128]{1,0:T(8,128)S(1)} %cholesky.194), custom_call_target="Cholesky" | custom-call | tf_op jit(solution)/shard_map/jit(cholesky)/cholesky | solution.py:95
  289.2 9.8 %custom-call.13 = f32[1,128,128]{1,2,0:T(8,128)S(1)} custom-call(f32[1,128,128]{2,1,0:T(8,128)S(1)} %get-tuple-element.74), custom_call_target="InvertDiagBlocksLowerTriangular" | custom-call | tf_op jit(solution)/shard_map/jit(cholesky)/cholesky | solution.py:95
  299.5 11.7 %cholesky.147 = f32[128,128]{1,0:T(8,128)S(1)} custom-call(f32[128,128]{1,0:T(8,128)S(1)} %convolution_subtract_fusion.3), custom_call_target="Cholesky" | custom-call | tf_op jit(solution)/shard_map/jit(cholesky)/cholesky | solution.py:95
  311.2 0.7 compare_reduce_fusion.2
  311.9 0.7 compare_reduce_fusion.3
  314.0 4.3 while.4
  314.2 0.7 fusion.77
  314.9 1.4 bitcast_dynamic-update-slice_fusion.4
  316.3 0.7 fusion.77
  316.9 1.4 bitcast_dynamic-update-slice_fusion.4
  318.3 19.7 %custom-call.14 = f32[2,128,128]{1,2,0:T(8,128)S(1)} custom-call(f32[2,128,128]{2,1,0:T(8,128)S(1)} %get-tuple-element.19), custom_call_target="InvertDiagBlocksLowerTriangular" | custom-call | tf_op jit(solution)/shard_map/triangular_solve/custom-call.0 | solution.py:96
  340.0 0.9 maximum_select_fusion
  340.9 1.2 or_select_fusion.3
  342.2 76.2 %all-reduce.12.cloned.1.call-done = f32[512,256]{0,1:T(8,128)} async-done(((f32[512,256]{0,1:T(8,128)}), f32[512,256]{0,1:T(8,128)}) %all-reduce.12.cloned.1.call-update) | async-done | bytes 524304 | tf_op jit(solution)/shard_map/psum | solution.py:20
  418.4 3.8 multiply_multiply_fusion.1
  422.3 1.1 dynamic-slice_select_fusion.1
  423.5 116.7 %all-reduce.18.cloned.1.call-done = (f32[1024,128]{0,1:T(8,128)}, f32[1024,128]{0,1:T(8,128)}) async-done(((f32[1024,128]{0,1:T(8,128)}, f32[1024,128]{0,1:T(8,128)}), (f32[1024,128]{0,1:T(8,128)}, f32[1024,128]{0,1:T(8,128)})) %all-reduce.18.cloned.1.call-update) | async-done | bytes 1048592 | tf_op jit(solution)/shard_map/psum | solution.py:20
  540.2 1.1 constant_dynamic-update-slice_fusion.5
  541.3 1.1 constant_dynamic-update-slice_fusion.4
  542.4 0.7 pad_maximum_fusion.5
  543.4 1.2 or_select_fusion
  544.7 1.2 or_select_fusion.1
  545.9 74.6 %all-reduce.14.cloned.1.call-done = f32[256,256]{0,1:T(8,128)} async-done(((f32[256,256]{0,1:T(8,128)}), f32[256,256]{0,1:T(8,128)}) %all-reduce.14.cloned.1.call-update) | async-done | bytes 262160 | tf_op jit(solution)/shard_map/psum | solution.py:94
  620.5 1.1 copy.15
  621.6 1.0 fusion.7
  622.6 11.7 %cholesky.164 = f32[128,128]{1,0:T(8,128)S(1)} custom-call(f32[128,128]{1,0:T(8,128)S(1)} %cholesky.197), custom_call_target="Cholesky" | custom-call | tf_op jit(solution)/shard_map/jit(cholesky)/cholesky | solution.py:95
  634.4 9.8 %custom-call.15 = f32[1,128,128]{1,2,0:T(8,128)S(1)} custom-call(f32[1,128,128]{2,1,0:T(8,128)S(1)} %get-tuple-element.70), custom_call_target="InvertDiagBlocksLowerTriangular" | custom-call | tf_op jit(solution)/shard_map/jit(cholesky)/cholesky | solution.py:95
  644.7 11.7 %cholesky.181 = f32[128,128]{1,0:T(8,128)S(1)} custom-call(f32[128,128]{1,0:T(8,128)S(1)} %convolution_subtract_fusion.2), custom_call_target="Cholesky" | custom-call | tf_op jit(solution)/shard_map/jit(cholesky)/cholesky | solution.py:95
  656.4 0.7 compare_reduce_fusion
  659.0 4.2 while.5
  659.9 1.3 bitcast_dynamic-update-slice_fusion.5
  661.9 1.3 bitcast_dynamic-update-slice_fusion.5
  663.3 19.7 %custom-call.16 = f32[2,128,128]{1,2,0:T(8,128)S(1)} custom-call(f32[2,128,128]{2,1,0:T(8,128)S(1)} %get-tuple-element.20), custom_call_target="InvertDiagBlocksLowerTriangular" | custom-call | tf_op jit(solution)/shard_map/triangular_solve/custom-call.0 | solution.py:96
  682.9 1.7 fusion.22
  684.6 1.7 convolution_subtract_fusion
  686.9 0.8 copy-done.2
  687.8 0.8 maximum_select_fusion.1
  688.8 0.7 fusion.19
  689.5 76.7 %all-reduce.16.cloned.1.call-done = f32[512,256]{0,1:T(8,128)} async-done(((f32[512,256]{0,1:T(8,128)}), f32[512,256]{0,1:T(8,128)}) %all-reduce.16.cloned.1.call-update) | async-done | bytes 524304 | tf_op jit(solution)/shard_map/psum | solution.py:20
  766.2 4.6 multiply_multiply_fusion
  770.8 2.9 copy.17
  (78 shorter events, 9.0 us)
Async XLA Ops:
  7.2 18.7 %copy-start.6 = (f32[1024]{0:T(1024)S(1)}, f32[1024]{0:T(1024)}, u32[]{:S(2)}) copy-start(f32[1024]{0:T(1024)} %param.10) | copy-start | bytes 12292
  7.2 187.8 %all-reduce.20.cloned.1.call-start = ((), (), s32[]{:S(2)}) async-start(), calls=%async_computation.5 | async-start | bytes 2097152 | tf_op jit(solution)/shard_map/psum | solution.py:20
  7.2 53.1 %collective-permute-start = (f32[1024,256]{1,0:T(8,128)}, f32[1024,256]{1,0:T(8,128)}, u32[]{:S(2)}, u32[]{:S(2)}) collective-permute-start(f32[1024,256]{1,0:T(8,128)} %param.9), channel_id=1, source_target_pairs={{0,64},{16,80},{32,96},{48,112},{64,0},{80,16},{96,32},{112,48},{1... | collective-permute-start | bytes 3145736 | tf_op jit(solution)/shard_map/ppermute | solution.py:15
  62.1 1.2 copy-start.5
  70.4 125.6 %copy-start = (f32[1024,512]{0,1:T(8,128)}, f32[1024,512]{0,1:T(8,128)S(1)}, u32[]{:S(2)}) copy-start(f32[1024,512]{0,1:T(8,128)S(1)} %copy.28) | copy-start | bytes 6291460
  71.6 203.7 %all-reduce.10.cloned.1.call-start = ((), (), s32[]{:S(2)}) async-start(), calls=%async_computation | async-start | bytes 524288 | tf_op jit(solution)/shard_map/psum | solution.py:94
  197.9 220.5 %all-reduce.12.cloned.1.call-start = ((), (), s32[]{:S(2)}) async-start(), calls=%async_computation.1 | async-start | bytes 1048576 | tf_op jit(solution)/shard_map/psum | solution.py:20
  208.7 129.3 %copy-start.4 = (f32[1024,128]{0,1:T(8,128)S(1)}, f32[1024,128]{0,1:T(8,128)}, u32[]{:S(2)}) copy-start(f32[1024,128]{0,1:T(8,128)} %get-tuple-element.45) | copy-start | bytes 1572868
  277.4 61.3 %copy-start.3 = (f32[1024,128]{0,1:T(8,128)S(1)}, f32[1024,128]{0,1:T(8,128)}, u32[]{:S(2)}) copy-start(f32[1024,128]{0,1:T(8,128)} %get-tuple-element.46) | copy-start | bytes 1572868
  339.9 82.4 %copy-start.1 = (f32[1024,128]{0,1:T(8,128)}, f32[1024,128]{0,1:T(8,128)S(1)}, u32[]{:S(2)}) copy-start(f32[1024,128]{0,1:T(8,128)S(1)} %fusion.25) | copy-start | bytes 1572868
  340.9 199.3 %all-reduce.18.cloned.1.call-start = ((), (), s32[]{:S(2)}) async-start(), calls=%async_computation.4 | async-start | bytes 2097152 | tf_op jit(solution)/shard_map/psum | solution.py:20
  423.3 197.2 %all-reduce.14.cloned.1.call-start = ((), (), s32[]{:S(2)}) async-start(), calls=%async_computation.2 | async-start | bytes 524288 | tf_op jit(solution)/shard_map/psum | solution.py:94
  543.1 223.1 %all-reduce.16.cloned.1.call-start = ((), (), s32[]{:S(2)}) async-start(), calls=%async_computation.3 | async-start | bytes 1048576 | tf_op jit(solution)/shard_map/psum | solution.py:20
  686.9 0.8 copy-start.2
Sparse Core Ops, SparseCore 0:
  71.7 123.1 all-reduce.19
  198.0 77.2 all-reduce.9
  341.0 77.3 all-reduce.11
  423.5 116.6 all-reduce.17
  543.3 77.2 all-reduce.13
  688.8 77.3 all-reduce.15
where the time goes:
time: 789 us; the launch traced here: 781 us
  waiting for transfers between devices  558 us (71%)
  other arithmetic  123 us (16%)
  between operations  37.4 us (5%)
  local copies, waits for them, and re-layouts  30.3 us (4%)
  matrix products  23.4 us (3%)
  starting transfers between devices  8.41 us (1%)
    psum x4, waiting for transfers between devices, broadcast(): return lax.psum(jnp.where(mine, shard, jnp.zeros_like(shard)), axis)  393 us
    psum x2, waiting for transfers between devices, per_device(): pivot_block = lax.psum(jnp.concatenate(owned_rows, axis=0), 'row')  135 us
    another operation x14, other arithmetic, per_device(): lower_factor = jnp.linalg.cholesky(pivot_block)  69.3 us
    another operation x7, other arithmetic, per_device(): lax.linalg.triangular_solve(lower_factor, panel_cols, left_side=False, lo...  39.6 us
    ppermute x1, waiting for transfers between devices, swapped(): lax.ppermute(shard, axis, [(i, i ^ 1 << bit) for i in range(lax.axis_size...  30 us
  transfers between devices with their start and end apart: 7, of which 7 were waited for; matrix products, arithmetic and copies ran while one was open for 2% of the time, Pallas kernels for 0%

commit v1 on v0

v1 whole, which is shorter than its diff:
```python
import jax
import jax.numpy as jnp
from jax import lax
from jax.experimental import pallas as pl
from jax.experimental.pallas import tpu as pltpu
from jax.sharding import PartitionSpec as P

F32 = jnp.float32
HIGHEST = lax.Precision.HIGHEST
MESH = pl.DeviceIdType.MESH
B = 128
LOWER = [4 * p + q for p in range(4) for q in range(p + 1)]


def dot(a, b, ca, cb):
    return lax.dot_general(
        a, b, (((ca,), (cb,)), ((), ())), precision=HIGHEST, preferred_element_type=F32
    )


def gather_kernel(
    pv, cm, con_ref, fd_ref, af_ref, pc_ref, pr_ref,
    cand, rsb, g, acand, ra, ab,
    ss_a, rs_a, ss_b, rs_b, ss_c, rs_c, ss_d, rs_d, ss_e, rs_e, ss_f, rs_f,
):
    f = lax.axis_index("front")
    r = lax.axis_index("row")
    c = lax.axis_index("col")
    s = r // 4
    d = r % 4

    def copy(src, dst, ssem, rsem, row, col):
        return pltpu.make_async_remote_copy(
            src_ref=src, dst_ref=dst, send_sem=ssem, recv_sem=rsem,
            device_id=(f, row, col), device_id_type=MESH,
        )

    barrier = pltpu.get_barrier_semaphore()
    for k in range(1, 8):
        pl.semaphore_signal(barrier, inc=1, device_id=(f, (r + k) % 8, c), device_id_type=MESH)
    for k in range(1, 16):
        pl.semaphore_signal(barrier, inc=1, device_id=(f, r, (c + k) % 16), device_id_type=MESH)

    cand[:, 64:72, :] = jnp.zeros((8, 8, 256), F32)
    for p in range(4):
        b = pv[p] % 32
        mine = jnp.logical_and(cm[s, b] == pv[p], b % 4 == d)
        rows = con_ref[pl.ds((b // 4) * B, B), :]
        rows = jnp.where(mine, rows, 0.0)
        cand[:, p * 16:(p + 1) * 16, :] = rows.reshape(8, 16, 256)
        line = fd_ref[pl.ds(pv[p] // 8, 1), :]
        line = jnp.where(pv[p] % 8 == r, line, 0.0)
        cand[:, 64 + p:65 + p, 0:B] = jnp.broadcast_to(line[None], (8, 1, B))
    rsb[r] = cand[r]

    pl.semaphore_wait(barrier, 22)

    first = []
    for k in range(1, 8):
        to = (r + k) % 8
        cp = copy(cand.at[to], rsb.at[r], ss_a.at[k], rs_a.at[r], to, c)
        cp.start()
        first.append(cp)
    for k in range(1, 8):
        frm = (r + 8 - k) % 8
        copy(cand.at[frm], rsb.at[frm], ss_a.at[k], rs_a.at[frm], frm, c).wait_recv()

    lane = lax.broadcasted_iota(jnp.int32, (16, B), 1)
    sub = lax.broadcasted_iota(jnp.int32, (16, B), 0)
    on_diag = lane == sub + 16 * r
    sums = []
    for ch in range(2):
        sums.append(
            (rsb[4 * ch, 0:64, :] + rsb[4 * ch + 1, 0:64, :])
            + (rsb[4 * ch + 2, 0:64, :] + rsb[4 * ch + 3, 0:64, :])
        )
    diag = rsb[0, 64:72, 0:B]
    for k in range(1, 8):
        diag = diag + rsb[k, 64:72, 0:B]
    for p in range(4):
        dp = jnp.where(on_diag, jnp.broadcast_to(diag[p:p + 1, :], (16, B)), 0.0)
        for l in range(4):
            i = l % 2
            total = jnp.where(16 * l + c == pv[p], dp, 0.0)
            for ch in range(2):
                here = cm[ch, 16 * i + c] == 16 * l + c
                part = sums[ch][p * 16:(p + 1) * 16, i * B:(i + 1) * B]
                total = total + jnp.where(here, part, 0.0)
            g[p, l] = total

    pc_ref[r] = g[...]
    gathers = []
    for k in range(1, 8):
        to = (r + k) % 8
        cp = copy(g, pc_ref.at[r], ss_e.at[k], rs_e.at[r], to, c)
        gathers.append(cp)

    for p in range(4):
        for q in range(p + 1):
            total = jnp.zeros((16, B), F32)
            for l in range(4):
                total = total + jnp.where(16 * l + c == pv[q], g[p, l], 0.0)
            acand[4 * p + q] = total
    for m in LOWER:
        @pl.when(c != m)
        def _():
            copy(acand.at[m], ra.at[c], ss_b.at[m], rs_b.at[c], r, m).start()

        @pl.when(c == m)
        def _():
            ra[m] = acand[m]
    for cp in gathers:
        cp.start()
    member = c % 4 <= c // 4

    @pl.when(member)
    def _():
        for n in range(16):
            @pl.when(c != n)
            def _():
                copy(acand.at[0], ra.at[n], ss_b.at[0], rs_b.at[n], r, n).wait_recv()
        ab[r] = jnp.sum(ra[...], axis=0)
        for k in range(1, 8):
            to = (r + k) % 8
            copy(ab.at[r], ab.at[r], ss_c.at[k], rs_c.at[r], to, c).start()
        for k in range(1, 8):
            frm = (r + 8 - k) % 8
            copy(ab.at[r], ab.at[frm], ss_c.at[k], rs_c.at[frm], frm, c).wait_recv()
        af_ref[c] = ab[...]
        for k in range(1, 16):
            to = (c + k) % 16
            copy(ab, af_ref.at[c], ss_d.at[k], rs_d.at[c], r, to).start()

    z = c // 2
    o = (z - r // 2 + 8) % 8
    relay = c % 2 == r % 2
    right = (c + 2) % 16
    left = (c + 14) % 16
    twin = c + 1 - 2 * (c % 2)

    def hop(h, k, src, do_right, do_left):
        @pl.when(do_right)
        def _():
            copy(src, pr_ref.at[h, k], ss_f.at[h, k, 0], rs_f.at[h, k], r, right).start()

        @pl.when(do_left)
        def _():
            copy(src, pr_ref.at[h, k], ss_f.at[h, k, 1], rs_f.at[h, k], r, left).start()

        copy(src, pr_ref.at[h, k], ss_f.at[h, k, 2], rs_f.at[h, k], r, twin).start()

    def wait_pr(h, k):
        copy(g, pr_ref.at[h, k], ss_f.at[h, k, 2], rs_f.at[h, k], r, twin).wait_recv()

    for k in range(8):
        @pl.when(r != k)
        def _():
            copy(g, pc_ref.at[k], ss_e.at[0], rs_e.at[k], r, c).wait_recv()

        @pl.when(relay)
        def _():
            for h in range(2):
                oh = (o + 8 - 4 * h) % 8

                @pl.when(oh == 0)
                def _():
                    pr_ref[h, k] = pc_ref[k]

                @pl.when(oh != 0)
                def _():
                    wait_pr(h, k)

                hop(h, k, pr_ref.at[h, k], oh <= 3, jnp.logical_or(oh == 0, oh >= 6))

    @pl.when(jnp.logical_not(relay))
    def _():
        for k in range(8):
            for h in range(2):
                wait_pr(h, k)

    for m in LOWER:
        @pl.when(c != m)
        def _():
            copy(ab, af_ref.at[m], ss_d.at[0], rs_d.at[m], r, m).wait_recv()
            copy(acand.at[m], ra.at[c], ss_b.at[m], rs_b.at[c], r, m).wait_send()
    for cp in first:
        cp.wait_send()
    for cp in gathers:
        cp.wait_send()

    @pl.when(member)
    def _():
        for k in range(1, 8):
            copy(ab.at[r], ab.at[r], ss_c.at[k], rs_c.at[r], (r + k) % 8, c).wait_send()
        for k in range(1, 16):
            copy(ab, af_ref.at[c], ss_d.at[k], rs_d.at[c], r, (c + k) % 16).wait_send()

    @pl.when(relay)
    def _():
        for k in range(8):
            for h in range(2):
                oh = (o + 8 - 4 * h) % 8

                @pl.when(oh <= 3)
                def _():
                    copy(g, pr_ref.at[h, k], ss_f.at[h, k, 0], rs_f.at[h, k], r, right).wait_send()

                @pl.when(jnp.logical_or(oh == 0, oh >= 6))
                def _():
                    copy(g, pr_ref.at[h, k], ss_f.at[h, k, 1], rs_f.at[h, k], r, left).wait_send()

                copy(g, pr_ref.at[h, k], ss_f.at[h, k, 2], rs_f.at[h, k], r, twin).wait_send()


def gather(pv, cm, contrib, fd):
    dma = pltpu.SemaphoreType.DMA
    vm = pl.BlockSpec(memory_space=pltpu.VMEM)
    sm = pl.BlockSpec(memory_space=pltpu.SMEM)
    return pl.pallas_call(
        gather_kernel,
        out_shape=(
            jax.ShapeDtypeStruct((16, 8, 16, B), F32),
            jax.ShapeDtypeStruct((8, 4, 4, 16, B), F32),
            jax.ShapeDtypeStruct((2, 8, 4, 4, 16, B), F32),
        ),
        in_specs=[sm, sm, vm, vm],
        out_specs=(vm, vm, vm),
        scratch_shapes=[
            pltpu.VMEM((8, 72, 256), F32),
            pltpu.VMEM((8, 72, 256), F32),
            pltpu.VMEM((4, 4, 16, B), F32),
            pltpu.VMEM((16, 16, B), F32),
            pltpu.VMEM((16, 16, B), F32),
            pltpu.VMEM((8, 16, B), F32),
            dma((8,)), dma((8,)), dma((16,)), dma((16,)), dma((8,)), dma((8,)),
            dma((16,)), dma((16,)), dma((8,)), dma((8,)), dma((2, 8, 3)), dma((2, 8)),
        ],
        compiler_params=pltpu.CompilerParams(
            collective_id=0, has_side_effects=True, vmem_limit_bytes=40 << 20
        ),
        name="gather",
    )(pv, cm, contrib, fd)


def factor_block(w_ref, r_ref, out_ref):
    row = lax.broadcasted_iota(jnp.int32, (16, 8, B), 0) * 8 + lax.broadcasted_iota(
        jnp.int32, (16, 8, B), 1
    )
    col = lax.broadcasted_iota(jnp.int32, (16, 8, B), 2)
    r_ref[...] = jnp.where(row == col, 1.0, 0.0).astype(F32)
    for t in range(16):
        w = w_ref[t]
        v = r_ref[t]
        cols = [jnp.broadcast_to(w[:, 8 * t + k:8 * t + k + 1], (8, B)) for k in range(8)]
        a = [[None] * 8 for _ in range(8)]
        for k in range(8):
            for i in range(k, 8):
                a[i][k] = jnp.broadcast_to(cols[k][i:i + 1, :], (8, B))
        wr = [jnp.broadcast_to(w[i:i + 1, :], (8, B)) for i in range(8)]
        vr = [jnp.broadcast_to(v[i:i + 1, :], (8, B)) for i in range(8)]
        rs = [None] * 8
        l = [[None] * 8 for _ in range(8)]
        for k in range(8):
            rs[k] = lax.rsqrt(a[k][k])
            for i in range(k + 1, 8):
                l[i][k] = a[i][k] * rs[k]
            for j in range(k + 1, 8):
                for i in range(j, 8):
                    a[i][j] = a[i][j] - l[i][k] * l[j][k]
            wr[k] = wr[k] * rs[k]
            vr[k] = vr[k] * rs[k]
            for i in range(k + 1, 8):
                wr[i] = wr[i] - l[i][k] * wr[k]
                vr[i] = vr[i] - l[i][k] * vr[k]
        for k in range(8):
            out_ref[8 * t + k:8 * t + k + 1, :] = vr[k][0:1, :]
        if t < 15:
            for k in range(7, -1, -1):
                for i in range(k + 1, 8):
                    wr[k] = wr[k] - l[i][k] * wr[i]
                    vr[k] = vr[k] - l[i][k] * vr[i]
                wr[k] = wr[k] * rs[k]
                vr[k] = vr[k] * rs[k]
            for u in range(t + 1, 16):
                old = w_ref[u]
                new = old
                inv = r_ref[u]
                for k in range(8):
                    factor = jnp.broadcast_to(old[:, 8 * t + k:8 * t + k + 1], (8, B))
                    new = new - factor * wr[k]
                    inv = inv - factor * vr[k]
                w_ref[u] = new
                r_ref[u] = inv


def cholesky_kernel(a_ref, l_ref, w_ref, r_ref):
    l_ref[...] = a_ref[...]

    def body(p, carry):
        w_ref[...] = l_ref[p, p].reshape(16, 8, B)
        factor_block(w_ref, r_ref, l_ref.at[p, p])
        inv = l_ref[p, p]

        def column(i, carry):
            @pl.when(i > p)
            def _():
                l_ref[i, p] = dot(l_ref[i, p], inv, 1, 1)
            return carry

        lax.fori_loop(0, 4, column, 0)

        def update(ij, carry):
            i = ij // 4
            j = ij % 4

            @pl.when(jnp.logical_and(j > p, i >= j))
            def _():
                l_ref[i, j] = l_ref[i, j] - dot(l_ref[i, p], l_ref[j, p], 1, 1)
            return carry

        lax.fori_loop(0, 16, update, 0)
        return carry

    lax.fori_loop(0, 4, body, 0)


def cholesky(a):
    vm = pl.BlockSpec(memory_space=pltpu.VMEM)
    return pl.pallas_call(
        cholesky_kernel,
        out_shape=jax.ShapeDtypeStruct((4, 4, B, B), F32),
        in_specs=[vm],
        out_specs=vm,
        scratch_shapes=[pltpu.VMEM((16, 8, B), F32)] * 2,
        name="cholesky",
        cost_estimate=pl.CostEstimate(flops=200_000_000, bytes_accessed=100_000_000, transcendentals=0),
    )(a)


def finish_kernel(pv, cm, pos, con_ref, x_ref, fd_ref, l_ref, pc_ref, pr_ref, lf_ref, s_ref, lt):
    r = pos[0]
    c = pos[1]
    s = r // 4
    for p in range(4):
        for k in range(8):
            blk = pr_ref[k % 2, :, p, k // 2].reshape(B, B)
            if p >= 2:
                gone = jnp.logical_or(8 * k + r == pv[0], 8 * k + r == pv[1])
                blk = jnp.where(gone, 0.0, blk)
            lt[p, :, k * B:(k + 1) * B] = blk
        for l in range(4):
            blk = pc_ref[:, p, l].reshape(B, B)
            lt[p, :, 1024 + l * B:1024 + (l + 1) * B] = blk
    for p in range(4):
        acc = lt[p]
        for q in range(p):
            acc = acc - dot(l_ref[p, q], lt[q], 1, 0)
        lt[p] = dot(l_ref[p, p], acc, 1, 0)
        if p >= 2:
            for k in range(8):
                gone = jnp.logical_or(8 * k + r == pv[0], 8 * k + r == pv[1])

                @pl.when(gone)
                def _():
                    lt[p, :, k * B:(k + 1) * B] = jnp.zeros((B, B), F32)
    mine = lt[c // 4, pl.ds(pl.multiple_of((c % 4) * 32, 32), 32), 0:1024]
    lf_ref[...] = mine.T
    row = lax.broadcasted_iota(jnp.int32, (B, B), 0)
    col = lax.broadcasted_iota(jnp.int32, (B, B), 1)
    for k in range(8):
        m = k % 4
        low = lt[:, :, k * B:(k + 1) * B].reshape(512, B)
        upd = dot(low, lt[:, :, 1024:1536].reshape(512, 512), 0, 0)
        own = con_ref[pl.ds(pl.multiple_of((2 * m + s) * B, B), B), :]
        other = x_ref[m]
        row_gone = jnp.zeros((), jnp.bool_)
        for p in range(4):
            row_gone = jnp.logical_or(row_gone, 8 * k + r == pv[p])
        own_row = cm[s, 8 * m + r] == 8 * k + r
        other_row = cm[1 - s, 8 * m + r] == 8 * k + r
        for l in range(4):
            i = l % 2
            front_col = 16 * l + c
            gone = row_gone
            for p in range(4):
                gone = jnp.logical_or(gone, front_col == pv[p])
            own_here = jnp.logical_and(own_row, cm[s, 16 * i + c] == front_col)
            other_here = jnp.logical_and(other_row, cm[1 - s, 16 * i + c] == front_col)
            tile = jnp.where(own_here, own[:, i * B:(i + 1) * B], 0.0)
            tile = tile + jnp.where(other_here, other[:, i * B:(i + 1) * B], 0.0)
            dk = jnp.where(row == col, jnp.broadcast_to(fd_ref[k:k + 1, :], (B, B)), 0.0)
            tile = tile + jnp.where(8 * k + r == front_col, dk, 0.0)
            tile = tile - upd[:, l * B:(l + 1) * B]
            s_ref[k * B:(k + 1) * B, l * B:(l + 1) * B] = jnp.where(gone, 0.0, tile)


def finish(pv, cm, pos, contrib, other, fd, low, pc, pr):
    vm = pl.BlockSpec(memory_space=pltpu.VMEM)
    sm = pl.BlockSpec(memory_space=pltpu.SMEM)
    return pl.pallas_call(
        finish_kernel,
        out_shape=(
            jax.ShapeDtypeStruct((1024, 32), F32),
            jax.ShapeDtypeStruct((1024, 512), F32),
        ),
        in_specs=[sm, sm, sm] + [vm] * 6,
        out_specs=(vm, vm),
        scratch_shapes=[pltpu.VMEM((4, B, 1536), F32)],
        compiler_params=pltpu.CompilerParams(vmem_limit_bytes=40 << 20),
        name="finish",
        cost_estimate=pl.CostEstimate(flops=1_000_000_000, bytes_accessed=8_000_000, transcendentals=0),
    )(pv, cm, pos, contrib, other, fd, low, pc, pr)


def per_device(contrib, front_diag, child_map, pivots):
    r = lax.axis_index("row")
    c = lax.axis_index("col")
    fd = front_diag.reshape(8, B)
    af, pc, pr = gather(pivots, child_map, contrib, fd)
    halves = contrib.reshape(4, 2, B, 256)
    away = lax.dynamic_index_in_dim(halves, 1 - r // 4, 1, keepdims=False)
    away, af = lax.optimization_barrier((away, af))
    other = lax.ppermute(away, "row", [(i, i ^ 4) for i in range(8)])
    low = cholesky(af.reshape(4, 4, B, B))
    pos = jnp.stack([r, c]).astype(jnp.int32)
    return finish(pivots, child_map, pos, contrib, other, fd, low, pc, pr)


def solution(mesh):
    placed = (P(("front", "row"), "col"), P(("front", "row")), P("front", None), P("front"))
    return jax.shard_map(
        per_device,
        mesh=mesh,
        in_specs=placed,
        out_specs=(P(("front", "row"), "col"), P(("front", "row"), "col")),
        check_vma=False,
    )
```

time: 789 us -> 393 us (0.50)
  waiting for transfers between devices: 558 us -> 0.01 us
  Pallas kernels: 0 us -> 375 us
  other arithmetic: 123 us -> 0.07 us
  between operations: 37.4 us -> 0.73 us
  matrix products: 23.4 us -> 0 us
  local copies, waits for them, and re-layouts: 30.3 us -> 12.3 us
    psum x6 -> x0, waiting for transfers between devices: 528 us -> none  [the longest x4 393 us: broadcast(): return lax.psum(jnp.where(mine, shard, jnp.zeros_like(shard)), axis)]
    pallas_call x0 -> x3, Pallas kernels: none -> 375 us  [the longest x1 332 us: gather(): pl.pallas_call(gather_kernel, out_shape=(jax.ShapeDtypeStruct((16, 8, 16,...]
    another operation x21 -> x1, other arithmetic: 109 us -> 0.07 us  [per_device(): pos = jnp.stack([r, c]).astype(jnp.int32)]
    ppermute x1, waiting for transfers between devices: 30 us -> 0.01 us  [per_device(): other = lax.ppermute(away, 'row', [(i, i ^ 4) for i in range(8)])]
    dot_general x6 -> x0, matrix products: 16.7 us -> none  [the longest x2 8.4 us: per_device(): update = jnp.einsum('ak,bk->ab', factor, across, precision=highest)]
    select_n x12 -> x0, other arithmetic: 8.87 us -> none  [the longest x4 3.99 us: broadcast(): return lax.psum(jnp.where(mine, shard, jnp.zeros_like(shard)), axis)]
    another operation x19 -> x0, local copies, waits for them, and re-layouts: 8.06 us -> none  [the longest x15 8.01 us: per_device(): lax.linalg.triangular_solve(lower_factor, panel_cols, left_side=False, lo...]
  transfers between devices with their start and end apart: 7 -> 1, of which waited for: 7 -> 0; matrix products, arithmetic and copies ran while one was open for 2% -> 0% of each run, Pallas kernels for 0% -> 8%
where the time goes in v1:
time: 393 us; the launch traced here: 390 us
  Pallas kernels  375 us (95%)
  local copies, waits for them, and re-layouts  12.3 us (3%)
    pallas_call x1, Pallas kernels, gather(): pl.pallas_call(gather_kernel, out_shape=(jax.ShapeDtypeStruct((16, 8, 16,...  332 us
    pallas_call x1, Pallas kernels, cholesky(): pl.pallas_call(cholesky_kernel, out_shape=jax.ShapeDtypeStruct((4, 4, B,...  29.6 us
    pallas_call x1, Pallas kernels, finish(): pl.pallas_call(finish_kernel, out_shape=(jax.ShapeDtypeStruct((1024, 32),...  13.7 us
    unnamed x26, local copies, waits for them, and re-layouts  8.44 us
  transfers between devices with their start and end apart: 1, of which 0 were waited for; matrix products, arithmetic and copies ran while one was open for 0% of the time, Pallas kernels for 8%

profile of v1, /device:TPU:6, one launch (start us, length us, event | category | flops | bytes accessed | tf_op | source)
XLA Modules:
  0.0 390.3 jit_solution(9954939550258266368)
XLA Ops:
  0.7 0.0 copy-start.8
  0.7 0.0 copy-start.1
  0.7 2.0 dynamic-slice_bitcast_fusion
  2.7 0.0 copy-start
  2.7 1.2 copy-done
  3.9 0.0 copy-start.7
  3.9 0.7 copy-done.7
  4.6 0.0 copy-start.9
  4.6 0.7 copy-done.9
  5.3 0.0 copy-start.11
  5.3 0.7 copy-done.11
  5.9 0.0 copy-start.10
  5.9 0.0 copy-start.12
  5.9 332.0 %gather.1 = (f32[16,8,16,128]{3,2,1,0:T(8,128)S(1)}, f32[8,4,4,16,128]{4,3,2,1,0:T(8,128)S(1)}, f32[2,8,4,4,16,128]{5,4,3,2,1,0:T(8,128)S(1)}) custom-call(s32[4]{0:T(128)S(1)} %copy-done.11, s32[2,32]{1,0:T(2,128)S(1)} %copy-done.9, f32[1024,256]{1,0:T(8,128)S(1)} %copy-done, f32[8,128]{1,0:T(8,128)S(1)} %bitcast.11), custom_call_target="tpu_custom_call" | custom-call | tf_op jit(solution)/shard_map/gather/pallas_call | solution.py:219
  338.0 0.0 copy-start.3
  338.0 1.0 copy-done.3
  338.9 0.0 copy-start.4
  338.9 1.0 copy-done.4
  339.9 1.9 collective-permute-start
  341.8 29.6 %cholesky.1.l_ref = f32[4,4,128,128]{3,2,1,0:T(8,128)} custom-call(f32[4,4,128,128]{3,2,1,0:T(8,128)} %bitcast.10), custom_call_target="tpu_custom_call" | custom-call | flops 200000000 | bytes 100000000 | tf_op jit(solution)/shard_map/cholesky/pallas_call | solution.py:329
  371.4 0.1 pad_add_fusion.pos
  371.5 0.0 collective-permute-done.x_ref
  371.5 0.0 copy-done.8
  371.5 0.0 copy-done.1
  371.5 0.0 copy-done.10
  371.5 0.0 copy-done.12
  371.5 0.0 copy-start.2
  371.5 1.2 copy-done.2
  372.7 0.0 copy-start.5
  372.7 1.2 copy-done.5
  374.0 13.7 %finish.1 = (f32[1024,32]{1,0:T(8,128)S(1)}, f32[1024,512]{1,0:T(8,128)}) custom-call(s32[4]{0:T(128)S(1)} %copy-done.12, s32[2,32]{1,0:T(2,128)S(1)} %copy-done.10, s32[2]{0:T(128)S(1)} %pad_add_fusion.pos, f32[1024,256]{1,0:T(8,128)S(1)} %copy-done.1, f32[4,128,256]{2,1,0:T(8,128)} %collective-permute-done.x_ref, f32[8,128]{1,0:T(8,128)S(1)} %bitcast.12, ...), custom_call_target="tpu_custom_call" | custom-call | flops 1000000000 | bytes 8000000 | tf_op jit(solution)/shard_map/finish/pallas_call | solution.py:400
  387.6 0.0 copy-start.6
  387.6 0.8 copy-done.6
  388.4 1.9 copy.7
Async XLA Ops:
  0.7 370.8 %copy-start.8 = (f32[1024]{0:T(1024)S(1)}, f32[1024]{0:T(1024)}, u32[]{:S(2)}) copy-start(f32[1024]{0:T(1024)} %param.5) | copy-start | bytes 12292
  0.7 370.8 %copy-start.1 = (f32[1024,256]{1,0:T(8,128)S(1)}, f32[1024,256]{1,0:T(8,128)}, u32[]{:S(2)}) copy-start(f32[1024,256]{1,0:T(8,128)} %con_ref.3) | copy-start | bytes 3145732
  2.7 1.2 copy-start
  3.9 0.7 copy-start.7
  4.6 0.7 copy-start.9
  5.3 0.7 copy-start.11
  5.9 365.6 %copy-start.10 = (s32[2,32]{1,0:T(2,128)S(1)}, s32[2,32]{1,0:T(2,128)}, u32[]{:S(2)}) copy-start(s32[2,32]{1,0:T(2,128)} %cm.3) | copy-start | bytes 772
  5.9 365.6 %copy-start.12 = (s32[4]{0:T(128)S(1)}, s32[4]{0:T(128)}, u32[]{:S(2)}) copy-start(s32[4]{0:T(128)} %pv.3) | copy-start | bytes 52
  338.0 1.0 copy-start.3
  338.9 1.0 copy-start.4
  339.9 31.6 %collective-permute-start = (f32[4,128,256]{2,1,0:T(8,128)}, f32[4,128,256]{2,1,0:T(8,128)}, u32[]{:S(2)}, u32[]{:S(2)}) collective-permute-start(f32[4,128,256]{2,1,0:T(8,128)} %dynamic-slice_bitcast_fusion), channel_id=1, source_target_pairs={{0,64},{16,80},{32,96},{48,112},{64,0},{80,16},{96,32},{112,48},{1... | collective-permute-start | bytes 1572872 | tf_op jit(solution)/shard_map/ppermute | solution.py:423
  371.5 1.2 copy-start.2
  372.7 1.2 copy-start.5
  387.6 0.8 copy-start.6

commit v2 on v1

--- a/solution.py
+++ b/solution.py
@@ -157,20 +157,27 @@
         def _():
             copy(g, pc_ref.at[k], ss_e.at[0], rs_e.at[k], r, c).wait_recv()
 
-        @pl.when(relay)
-        def _():
+    @pl.when(relay)
+    def _():
+        for h in range(2):
+            oh = (o + 8 - 4 * h) % 8
+
+            @pl.when(oh == 0)
+            def _():
+                pr_ref[h] = pc_ref[...]
+        for step in range(12):
             for h in range(2):
                 oh = (o + 8 - 4 * h) % 8
-
-                @pl.when(oh == 0)
+                far = jnp.where(oh <= 4, oh, 8 - oh)
+                k = step - far
+
+                @pl.when(jnp.logical_and(k >= 0, k < 8))
                 def _():
-                    pr_ref[h, k] = pc_ref[k]
-
-                @pl.when(oh != 0)
-                def _():
-                    wait_pr(h, k)
-
-                hop(h, k, pr_ref.at[h, k], oh <= 3, jnp.logical_or(oh == 0, oh >= 6))
+                    @pl.when(oh != 0)
+                    def _():
+                        wait_pr(h, k)
+
+                    hop(h, k, pr_ref.at[h, k], oh <= 3, jnp.logical_or(oh == 0, oh >= 6))
 
     @pl.when(jnp.logical_not(relay))
     def _():

time: 393 us -> 176 us (0.45)
  Pallas kernels: 375 us -> 159 us
    pallas_call x1, Pallas kernels: 332 us -> 116 us  [gather(): pl.pallas_call(gather_kernel, out_shape=(jax.ShapeDtypeStruct((16, 8, 16,...]
  transfers between devices with their start and end apart: 1 -> 1, of which waited for: 0 -> 0; matrix products, arithmetic and copies ran while one was open for 0% -> 0% of each run, Pallas kernels for 8% -> 17%
where the time goes in v2:
time: 176 us; the launch traced here: 174 us
  Pallas kernels  159 us (90%)
  local copies, waits for them, and re-layouts  12.3 us (7%)
  starting transfers between devices  1.91 us (1%)
    pallas_call x1, Pallas kernels, gather(): pl.pallas_call(gather_kernel, out_shape=(jax.ShapeDtypeStruct((16, 8, 16,...  116 us
    pallas_call x1, Pallas kernels, cholesky(): pl.pallas_call(cholesky_kernel, out_shape=jax.ShapeDtypeStruct((4, 4, B,...  29.6 us
    pallas_call x1, Pallas kernels, finish(): pl.pallas_call(finish_kernel, out_shape=(jax.ShapeDtypeStruct((1024, 32),...  13.7 us
    unnamed x26, local copies, waits for them, and re-layouts  8.44 us
  transfers between devices with their start and end apart: 1, of which 0 were waited for; matrix products, arithmetic and copies ran while one was open for 0% of the time, Pallas kernels for 17%

profile of v2, /device:TPU:6, one launch (start us, length us, event | category | flops | bytes accessed | tf_op | source)
XLA Modules:
  0.0 174.1 jit_solution(15789544573386152910)
XLA Ops:
  0.7 0.0 copy-start.8
  0.7 0.0 copy-start.1
  0.7 2.0 %dynamic-slice_bitcast_fusion = f32[4,128,256]{2,1,0:T(8,128)} fusion(f32[4,2,128,256]{3,2,1,0:T(8,128)} %bitcast.9, s32[]{:T(128)S(6)} %select_n.10), kind=kLoop, calls=%fused_computation | loop fusion | bytes 1048580 | tf_op jit(solution)/shard_map/jit(dynamic_index_in_dim)/squeeze | solution.py:428
  2.7 0.0 copy-start
  2.7 1.2 copy-done
  3.9 0.0 copy-start.7
  3.9 0.7 copy-done.7
  4.6 0.0 copy-start.9
  4.6 0.7 copy-done.9
  5.3 0.0 copy-start.11
  5.3 0.7 copy-done.11
  5.9 0.0 copy-start.10
  5.9 0.0 copy-start.12
  5.9 115.8 %gather.1 = (f32[16,8,16,128]{3,2,1,0:T(8,128)S(1)}, f32[8,4,4,16,128]{4,3,2,1,0:T(8,128)S(1)}, f32[2,8,4,4,16,128]{5,4,3,2,1,0:T(8,128)S(1)}) custom-call(s32[4]{0:T(128)S(1)} %copy-done.11, s32[2,32]{1,0:T(2,128)S(1)} %copy-done.9, f32[1024,256]{1,0:T(8,128)S(1)} %copy-done, f32[8,128]{1,0:T(8,128)S(1)} %bitcast.11), custom_call_target="tpu_custom_call" | custom-call | tf_op jit(solution)/shard_map/gather/pallas_call | solution.py:226
  121.7 0.0 copy-start.3
  121.8 1.0 copy-done.3
  122.7 0.0 copy-start.4
  122.7 1.0 copy-done.4
  123.7 1.9 %collective-permute-start = (f32[4,128,256]{2,1,0:T(8,128)}, f32[4,128,256]{2,1,0:T(8,128)}, u32[]{:S(2)}, u32[]{:S(2)}) collective-permute-start(f32[4,128,256]{2,1,0:T(8,128)} %dynamic-slice_bitcast_fusion), channel_id=1, source_target_pairs={{0,64},{16,80},{32,96},{48,112},{64,0},{80,16},{96,32},{112,48},{1... | collective-permute-start | bytes 1572872 | tf_op jit(solution)/shard_map/ppermute | solution.py:430
  125.6 29.6 %cholesky.1.l_ref = f32[4,4,128,128]{3,2,1,0:T(8,128)} custom-call(f32[4,4,128,128]{3,2,1,0:T(8,128)} %bitcast.10), custom_call_target="tpu_custom_call" | custom-call | flops 200000000 | bytes 100000000 | tf_op jit(solution)/shard_map/cholesky/pallas_call | solution.py:336
  155.2 0.1 pad_add_fusion.pos
  155.3 0.0 collective-permute-done.x_ref
  155.3 0.0 copy-done.8
  155.3 0.0 copy-done.1
  155.3 0.0 copy-done.10
  155.3 0.0 copy-done.12
  155.3 0.0 copy-start.2
  155.3 1.2 copy-done.2
  156.5 0.0 copy-start.5
  156.5 1.2 copy-done.5
  157.7 13.7 %finish.1 = (f32[1024,32]{1,0:T(8,128)S(1)}, f32[1024,512]{1,0:T(8,128)}) custom-call(s32[4]{0:T(128)S(1)} %copy-done.12, s32[2,32]{1,0:T(2,128)S(1)} %copy-done.10, s32[2]{0:T(128)S(1)} %pad_add_fusion.pos, f32[1024,256]{1,0:T(8,128)S(1)} %copy-done.1, f32[4,128,256]{2,1,0:T(8,128)} %collective-permute-done.x_ref, f32[8,128]{1,0:T(8,128)S(1)} %bitcast.12, ...), custom_call_target="tpu_custom_call" | custom-call | flops 1000000000 | bytes 8000000 | tf_op jit(solution)/shard_map/finish/pallas_call | solution.py:407
  171.4 0.0 copy-start.6
  171.4 0.8 copy-done.6
  172.2 1.9 %copy.7 = f32[1024,32]{0,1:T(8,128)} copy(f32[1024,32]{1,0:T(8,128)} %copy-done.6) | data formatting | bytes 262144 | tf_op jit(solution)/shard_map/finish/pallas_call | solution.py:407
Async XLA Ops:
  0.7 154.6 %copy-start.8 = (f32[1024]{0:T(1024)S(1)}, f32[1024]{0:T(1024)}, u32[]{:S(2)}) copy-start(f32[1024]{0:T(1024)} %param.5) | copy-start | bytes 12292
  0.7 154.6 %copy-start.1 = (f32[1024,256]{1,0:T(8,128)S(1)}, f32[1024,256]{1,0:T(8,128)}, u32[]{:S(2)}) copy-start(f32[1024,256]{1,0:T(8,128)} %con_ref.3) | copy-start | bytes 3145732
  2.7 1.2 copy-start
  3.9 0.7 copy-start.7
  4.6 0.7 copy-start.9
  5.3 0.7 copy-start.11
  5.9 149.4 %copy-start.10 = (s32[2,32]{1,0:T(2,128)S(1)}, s32[2,32]{1,0:T(2,128)}, u32[]{:S(2)}) copy-start(s32[2,32]{1,0:T(2,128)} %cm.3) | copy-start | bytes 772
  5.9 149.4 %copy-start.12 = (s32[4]{0:T(128)S(1)}, s32[4]{0:T(128)}, u32[]{:S(2)}) copy-start(s32[4]{0:T(128)} %pv.3) | copy-start | bytes 52
  121.7 1.0 copy-start.3
  122.7 1.0 copy-start.4
  123.7 31.6 %collective-permute-start = (f32[4,128,256]{2,1,0:T(8,128)}, f32[4,128,256]{2,1,0:T(8,128)}, u32[]{:S(2)}, u32[]{:S(2)}) collective-permute-start(f32[4,128,256]{2,1,0:T(8,128)} %dynamic-slice_bitcast_fusion), channel_id=1, source_target_pairs={{0,64},{16,80},{32,96},{48,112},{64,0},{80,16},{96,32},{112,48},{1... | collective-permute-start | bytes 1572872 | tf_op jit(solution)/shard_map/ppermute | solution.py:430
  155.3 1.2 copy-start.2
  156.5 1.2 copy-start.5
  171.4 0.8 copy-start.6

commit v3 on v1

v3 whole, which is shorter than its diff:
```python
import jax
import jax.numpy as jnp
from jax import lax
from jax.experimental import pallas as pl
from jax.experimental.pallas import tpu as pltpu
from jax.sharding import PartitionSpec as P

F32 = jnp.float32
HIGHEST = lax.Precision.HIGHEST
MESH = pl.DeviceIdType.MESH
B = 128


def dot(a, b, ca, cb):
    return lax.dot_general(
        a, b, (((ca,), (cb,)), ((), ())), precision=HIGHEST, preferred_element_type=F32
    )


def factor_block(w_ref, r_ref, out_ref, tick):
    row = lax.broadcasted_iota(jnp.int32, (16, 8, B), 0) * 8 + lax.broadcasted_iota(
        jnp.int32, (16, 8, B), 1
    )
    col = lax.broadcasted_iota(jnp.int32, (16, 8, B), 2)
    r_ref[...] = jnp.where(row == col, 1.0, 0.0).astype(F32)
    for t in range(16):
        tick(t)
        w = w_ref[t]
        v = r_ref[t]
        cols = [jnp.broadcast_to(w[:, 8 * t + k:8 * t + k + 1], (8, B)) for k in range(8)]
        a = [[None] * 8 for _ in range(8)]
        for k in range(8):
            for i in range(k, 8):
                a[i][k] = jnp.broadcast_to(cols[k][i:i + 1, :], (8, B))
        wr = [jnp.broadcast_to(w[i:i + 1, :], (8, B)) for i in range(8)]
        vr = [jnp.broadcast_to(v[i:i + 1, :], (8, B)) for i in range(8)]
        rs = [None] * 8
        l = [[None] * 8 for _ in range(8)]
        for k in range(8):
            rs[k] = lax.rsqrt(a[k][k])
            for i in range(k + 1, 8):
                l[i][k] = a[i][k] * rs[k]
            for j in range(k + 1, 8):
                for i in range(j, 8):
                    a[i][j] = a[i][j] - l[i][k] * l[j][k]
            wr[k] = wr[k] * rs[k]
            vr[k] = vr[k] * rs[k]
            for i in range(k + 1, 8):
                wr[i] = wr[i] - l[i][k] * wr[k]
                vr[i] = vr[i] - l[i][k] * vr[k]
        for k in range(8):
            out_ref[8 * t + k:8 * t + k + 1, :] = vr[k][0:1, :]
        if t < 15:
            for k in range(7, -1, -1):
                for i in range(k + 1, 8):
                    wr[k] = wr[k] - l[i][k] * wr[i]
                    vr[k] = vr[k] - l[i][k] * vr[i]
                wr[k] = wr[k] * rs[k]
                vr[k] = vr[k] * rs[k]
            for u in range(t + 1, 16):
                old = w_ref[u]
                new = old
                inv = r_ref[u]
                for k in range(8):
                    factor = jnp.broadcast_to(old[:, 8 * t + k:8 * t + k + 1], (8, B))
                    new = new - factor * wr[k]
                    inv = inv - factor * vr[k]
                w_ref[u] = new
                r_ref[u] = inv


def factor_kernel(
    pv, cm, con_ref, fd_ref, l_ref, pc_ref, pr_ref, x_ref,
    cand, rsb, acand, za, af, w_ref, r_ref,
    ss_a, rs_a, ss_b, rs_b, ss_c, rs_c, ss_e, rs_e, ss_f, rs_f, ss_x, rs_x,
):
    f = lax.axis_index("front")
    r = lax.axis_index("row")
    c = lax.axis_index("col")
    s = r // 4
    d = r % 4

    def copy(src, dst, ssem, rsem, row, col):
        return pltpu.make_async_remote_copy(
            src_ref=src, dst_ref=dst, send_sem=ssem, recv_sem=rsem,
            device_id=(f, row, col), device_id_type=MESH,
        )

    barrier = pltpu.get_barrier_semaphore()
    for k in range(1, 8):
        pl.semaphore_signal(barrier, inc=1, device_id=(f, (r + k) % 8, c), device_id_type=MESH)
    for k in range(1, 16):
        pl.semaphore_signal(barrier, inc=1, device_id=(f, r, (c + k) % 16), device_id_type=MESH)

    cand[:, 0:8, :] = jnp.zeros((8, 8, 256), F32)
    for p in range(4):
        b = pv[p] % 32
        mine = jnp.logical_and(cm[s, b] == pv[p], b % 4 == d)
        rows = con_ref[pl.ds((b // 4) * B, B), :]
        rows = jnp.where(mine, rows, 0.0)
        cand[:, 8 + p * 16:24 + p * 16, :] = rows.reshape(8, 16, 256)
        line = fd_ref[pl.ds(pv[p] // 8, 1), :]
        line = jnp.where(pv[p] % 8 == r, line, 0.0)
        cand[:, p:p + 1, 0:B] = jnp.broadcast_to(line[None], (8, 1, B))
    rsb[r] = cand[r]

    pl.semaphore_wait(barrier, 22)

    def span(p):
        return pl.ds(0, 24) if p == 0 else pl.ds(8 + 16 * p, 16)

    def rs_copy(p, k):
        to = (r + k) % 8
        return copy(cand.at[to, span(p)], rsb.at[r, span(p)], ss_a.at[p, k], rs_a.at[p, r], to, c)

    for p in range(4):
        for k in range(1, 8):
            rs_copy(p, k).start()

    lane = lax.broadcasted_iota(jnp.int32, (16, B), 1)
    sub = lax.broadcasted_iota(jnp.int32, (16, B), 0)
    on_diag = lane == sub + 16 * r

    def z_copy(p, k):
        to = (c + k) % 16
        return copy(
            acand.at[p, pl.ds(0, p + 1)], za.at[p, c, pl.ds(0, p + 1)],
            ss_b.at[p, k], rs_b.at[p, c], r, to,
        )

    def stage_z(p):
        for k in range(1, 8):
            frm = (r + k) % 8
            copy(
                cand.at[frm, span(p)], rsb.at[frm, span(p)], ss_a.at[p, k], rs_a.at[p, frm], frm, c
            ).wait_recv()
        rows = [rsb[n, 8 + 16 * p:24 + 16 * p, :] for n in range(8)]
        sums = [
            (rows[4 * ch] + rows[4 * ch + 1]) + (rows[4 * ch + 2] + rows[4 * ch + 3])
            for ch in range(2)
        ]
        diag = jnp.sum(rsb[:, p:p + 1, 0:B], axis=0)
        dp = jnp.where(on_diag, jnp.broadcast_to(diag, (16, B)), 0.0)
        parts = []
        for l in range(4):
            i = l % 2
            total = jnp.where(16 * l + c == pv[p], dp, 0.0)
            for ch in range(2):
                here = cm[ch, 16 * i + c] == 16 * l + c
                total = total + jnp.where(here, sums[ch][:, i * B:(i + 1) * B], 0.0)
            pc_ref[r, p, l] = total
            parts.append(total)
        for q in range(p + 1):
            total = jnp.zeros((16, B), F32)
            for l in range(4):
                total = total + jnp.where(16 * l + c == pv[q], parts[l], 0.0)
            acand[p, q] = total
            za[p, c, q] = total
        for k in range(1, 16):
            z_copy(p, k).start()

    def y_copy(p, k):
        to = (r + k) % 8
        here = af.at[p, r, pl.ds(0, p + 1)]
        return copy(here, here, ss_c.at[p, k], rs_c.at[p, r], to, c)

    def stage_y(p):
        for k in range(1, 16):
            frm = (c + k) % 16
            copy(
                acand.at[p, pl.ds(0, p + 1)], za.at[p, frm, pl.ds(0, p + 1)],
                ss_b.at[p, k], rs_b.at[p, frm], r, frm,
            ).wait_recv()
        af[p, r, 0:p + 1] = jnp.sum(za[p, :, 0:p + 1], axis=0)
        for k in range(1, 8):
            y_copy(p, k).start()

    def stage_a(p):
        for k in range(1, 8):
            frm = (r + k) % 8
            there = af.at[p, frm, pl.ds(0, p + 1)]
            copy(there, there, ss_c.at[p, k], rs_c.at[p, frm], frm, c).wait_recv()

    def ring(step, way):
        origin = (r + (8 - step + 1 if way == 0 else step - 1)) % 8
        to = (r + (1 if way == 0 else 7)) % 8
        chunk = pc_ref.at[origin]
        return copy(chunk, chunk, ss_e.at[way, step], rs_e.at[origin], to, c)

    def ring_recv(origin):
        chunk = pc_ref.at[origin]
        copy(chunk, chunk, ss_e.at[0, 1], rs_e.at[origin], r, c).wait_recv()

    def stage_ring(step):
        if step > 1:
            ring_recv((r + 8 - step + 1) % 8)
            if step <= 4:
                ring_recv((r + step - 1) % 8)
        if step <= 4:
            ring(step, 0).start()
        if step <= 3:
            ring(step, 1).start()

    z = c // 2
    o = (z - r // 2 + 8) % 8
    relay = c % 2 == r % 2
    right = (c + 2) % 16
    left = (c + 14) % 16
    twin = c + 1 - 2 * (c % 2)

    def relay_copy(h, n, way):
        chunk = pr_ref.at[h, n]
        to = (right, left, twin)[way]
        return copy(chunk, chunk, ss_f.at[h, n, way], rs_f.at[h, n], r, to)

    def ways(h):
        oh = (o + 8 - 4 * h) % 8
        return oh, oh <= 3, jnp.logical_or(oh == 0, oh >= 6)

    def stage_relay(step):
        @pl.when(relay)
        def _():
            for h in range(2):
                oh, go_right, go_left = ways(h)
                j = step - jnp.where(oh <= 4, oh, 8 - oh)
                n = (r + jnp.where(j % 2 == 0, j // 2, 8 - (j + 1) // 2)) % 8

                @pl.when(jnp.logical_and(j >= 0, j < 8))
                def _():
                    @pl.when(oh == 0)
                    def _():
                        pr_ref[h, n] = pc_ref[n]

                    @pl.when(oh != 0)
                    def _():
                        relay_copy(h, n, 2).wait_recv()

                    @pl.when(go_right)
                    def _():
                        relay_copy(h, n, 0).start()

                    @pl.when(go_left)
                    def _():
                        relay_copy(h, n, 1).start()

                    relay_copy(h, n, 2).start()

    def x_copy(m):
        rows = pl.ds((2 * m + 1 - s) * B, B)
        return copy(con_ref.at[rows], x_ref.at[m], ss_x.at[m], rs_x.at[m], (r + 4) % 8, c)

    stage_z(0)
    stage_z(1)
    stage_z(2)
    stage_y(0)
    stage_z(3)
    stage_ring(1)
    stage_relay(0)
    stage_y(1)

    actions = {
        2: [lambda: stage_ring(2), lambda: stage_relay(1)],
        8: [lambda: stage_relay(2)],
        10: [lambda: stage_y(2)],
        11: [lambda: stage_ring(3)],
        13: [lambda: x_copy(0).start()],
        14: [lambda: stage_relay(3)],
        19: [lambda: x_copy(1).start()],
        20: [lambda: stage_ring(4), lambda: stage_relay(4)],
        25: [lambda: x_copy(2).start()],
        26: [lambda: stage_relay(5)],
        28: [lambda: stage_y(3)],
        29: [lambda: stage_ring(5)],
        31: [lambda: x_copy(3).start()],
        32: [lambda: stage_relay(6)],
        38: [lambda: stage_relay(7)],
        44: [lambda: stage_relay(8)],
        50: [lambda: stage_relay(9)],
        56: [lambda: stage_relay(10)],
        62: [lambda: stage_relay(11)],
    }

    def block(p, carry):
        for n in range(4):
            @pl.when(p == n)
            def _():
                stage_a(n)

        def left_block(q, carry):
            def minus(j, acc):
                return acc - dot(l_ref[p, j], l_ref[q, j], 1, 1)

            acc = lax.fori_loop(0, q, minus, af[p, :, q].reshape(B, B))
            l_ref[p, q] = dot(acc, l_ref[q, q], 1, 1)
            return carry

        lax.fori_loop(0, p, left_block, 0)

        def minus(j, acc):
            low = l_ref[p, j]
            return acc - dot(low, low, 1, 1)

        acc = lax.fori_loop(0, p, minus, af[p, :, p].reshape(B, B))
        w_ref[...] = acc.reshape(16, 8, B)

        def tick(t):
            for n in range(4):
                if 16 * n + t in actions:
                    @pl.when(p == n)
                    def _():
                        for act in actions[16 * n + t]:
                            act()

        factor_block(w_ref, r_ref, l_ref.at[p, p], tick)
        return carry

    lax.fori_loop(0, 4, block, 0)

    for m in range(4):
        x_copy(m).wait()

    @pl.when(jnp.logical_not(relay))
    def _():
        for h in range(2):
            for n in range(8):
                relay_copy(h, n, 2).wait_recv()

    @pl.when(relay)
    def _():
        for h in range(2):
            _, go_right, go_left = ways(h)
            for n in range(8):
                @pl.when(go_right)
                def _():
                    relay_copy(h, n, 0).wait_send()

                @pl.when(go_left)
                def _():
                    relay_copy(h, n, 1).wait_send()

                relay_copy(h, n, 2).wait_send()
    for step in range(1, 5):
        ring(step, 0).wait_send()
        if step <= 3:
            ring(step, 1).wait_send()
    for p in range(4):
        for k in range(1, 8):
            rs_copy(p, k).wait_send()
            y_copy(p, k).wait_send()
        for k in range(1, 16):
            z_copy(p, k).wait_send()


def factor(pv, cm, contrib, fd):
    dma = pltpu.SemaphoreType.DMA
    vm = pl.BlockSpec(memory_space=pltpu.VMEM)
    sm = pl.BlockSpec(memory_space=pltpu.SMEM)
    return pl.pallas_call(
        factor_kernel,
        out_shape=(
            jax.ShapeDtypeStruct((4, 4, B, B), F32),
            jax.ShapeDtypeStruct((8, 4, 4, 16, B), F32),
            jax.ShapeDtypeStruct((2, 8, 4, 4, 16, B), F32),
            jax.ShapeDtypeStruct((4, B, 256), F32),
        ),
        in_specs=[sm, sm, vm, vm],
        out_specs=(vm, vm, vm, vm),
        scratch_shapes=[
            pltpu.VMEM((8, 72, 256), F32),
            pltpu.VMEM((8, 72, 256), F32),
            pltpu.VMEM((4, 4, 16, B), F32),
            pltpu.VMEM((4, 16, 4, 16, B), F32),
            pltpu.VMEM((4, 8, 4, 16, B), F32),
            pltpu.VMEM((16, 8, B), F32),
            pltpu.VMEM((16, 8, B), F32),
            dma((4, 8)), dma((4, 8)), dma((4, 16)), dma((4, 16)), dma((4, 8)), dma((4, 8)),
            dma((2, 5)), dma((8,)), dma((2, 8, 3)), dma((2, 8)), dma((4,)), dma((4,)),
        ],
        compiler_params=pltpu.CompilerParams(
            collective_id=0, has_side_effects=True, vmem_limit_bytes=20 << 20
        ),
        name="factor",
        cost_estimate=pl.CostEstimate(flops=200_000_000, bytes_accessed=10_000_000, transcendentals=0),
    )(pv, cm, contrib, fd)


def finish_kernel(pv, cm, pos, con_ref, x_ref, fd_ref, l_ref, pc_ref, pr_ref, lf_ref, s_ref, lt):
    r = pos[0]
    c = pos[1]
    s = r // 4
    for p in range(4):
        for k in range(8):
            blk = pr_ref[k % 2, :, p, k // 2].reshape(B, B)
            if p >= 2:
                gone = jnp.logical_or(8 * k + r == pv[0], 8 * k + r == pv[1])
                blk = jnp.where(gone, 0.0, blk)
            lt[p, :, k * B:(k + 1) * B] = blk
        for l in range(4):
            blk = pc_ref[:, p, l].reshape(B, B)
            lt[p, :, 1024 + l * B:1024 + (l + 1) * B] = blk
    for p in range(4):
        acc = lt[p]
        for q in range(p):
            acc = acc - dot(l_ref[p, q], lt[q], 1, 0)
        lt[p] = dot(l_ref[p, p], acc, 1, 0)
        if p >= 2:
            for k in range(8):
                gone = jnp.logical_or(8 * k + r == pv[0], 8 * k + r == pv[1])

                @pl.when(gone)
                def _():
                    lt[p, :, k * B:(k + 1) * B] = jnp.zeros((B, B), F32)
    mine = lt[c // 4, pl.ds(pl.multiple_of((c % 4) * 32, 32), 32), 0:1024]
    lf_ref[...] = mine.T
    row = lax.broadcasted_iota(jnp.int32, (B, B), 0)
    col = lax.broadcasted_iota(jnp.int32, (B, B), 1)
    for k in range(8):
        m = k % 4
        low = lt[:, :, k * B:(k + 1) * B].reshape(512, B)
        upd = dot(low, lt[:, :, 1024:1536].reshape(512, 512), 0, 0)
        own = con_ref[pl.ds(pl.multiple_of((2 * m + s) * B, B), B), :]
        other = x_ref[m]
        row_gone = jnp.zeros((), jnp.bool_)
        for p in range(4):
            row_gone = jnp.logical_or(row_gone, 8 * k + r == pv[p])
        own_row = cm[s, 8 * m + r] == 8 * k + r
        other_row = cm[1 - s, 8 * m + r] == 8 * k + r
        for l in range(4):
            i = l % 2
            front_col = 16 * l + c
            gone = row_gone
            for p in range(4):
                gone = jnp.logical_or(gone, front_col == pv[p])
            own_here = jnp.logical_and(own_row, cm[s, 16 * i + c] == front_col)
            other_here = jnp.logical_and(other_row, cm[1 - s, 16 * i + c] == front_col)
            tile = jnp.where(own_here, own[:, i * B:(i + 1) * B], 0.0)
            tile = tile + jnp.where(other_here, other[:, i * B:(i + 1) * B], 0.0)
            dk = jnp.where(row == col, jnp.broadcast_to(fd_ref[k:k + 1, :], (B, B)), 0.0)
            tile = tile + jnp.where(8 * k + r == front_col, dk, 0.0)
            tile = tile - upd[:, l * B:(l + 1) * B]
            s_ref[k * B:(k + 1) * B, l * B:(l + 1) * B] = jnp.where(gone, 0.0, tile)


def finish(pv, cm, pos, contrib, other, fd, low, pc, pr):
    vm = pl.BlockSpec(memory_space=pltpu.VMEM)
    sm = pl.BlockSpec(memory_space=pltpu.SMEM)
    return pl.pallas_call(
        finish_kernel,
        out_shape=(
            jax.ShapeDtypeStruct((1024, 32), F32),
            jax.ShapeDtypeStruct((1024, 512), F32),
        ),
        in_specs=[sm, sm, sm] + [vm] * 6,
        out_specs=(vm, vm),
        scratch_shapes=[pltpu.VMEM((4, B, 1536), F32)],
        compiler_params=pltpu.CompilerParams(vmem_limit_bytes=24 << 20),
        name="finish",
        cost_estimate=pl.CostEstimate(flops=1_000_000_000, bytes_accessed=8_000_000, transcendentals=0),
    )(pv, cm, pos, contrib, other, fd, low, pc, pr)


def per_device(contrib, front_diag, child_map, pivots):
    r = lax.axis_index("row")
    c = lax.axis_index("col")
    fd = front_diag.reshape(8, B)
    low, pc, pr, other = factor(pivots, child_map, contrib, fd)
    pos = jnp.stack([r, c]).astype(jnp.int32)
    return finish(pivots, child_map, pos, contrib, other, fd, low, pc, pr)


def solution(mesh):
    placed = (P(("front", "row"), "col"), P(("front", "row")), P("front", None), P("front"))
    return jax.shard_map(
        per_device,
        mesh=mesh,
        in_specs=placed,
        out_specs=(P(("front", "row"), "col"), P(("front", "row"), "col")),
        check_vma=False,
    )
```

time: 393 us -> 136 us (0.35)
  Pallas kernels: 375 us -> 127 us
  local copies, waits for them, and re-layouts: 12.3 us -> 6.63 us
    pallas_call x2 -> x1, Pallas kernels: 362 us -> 114 us  [factor(): pl.pallas_call(factor_kernel, out_shape=(jax.ShapeDtypeStruct((4, 4, B, B...]
    unnamed x26 -> x14, local copies, waits for them, and re-layouts: 8.44 us -> 5.8 us
  transfers between devices with their start and end apart: 1 -> 0, of which waited for: 0 -> 0; matrix products, arithmetic and copies ran while one was open for 0% -> 0% of each run, Pallas kernels for 8% -> 0%
where the time goes in v3:
time: 136 us; the launch traced here: 135 us
  Pallas kernels  127 us (93%)
  local copies, waits for them, and re-layouts  6.63 us (5%)
    pallas_call x1, Pallas kernels, factor(): pl.pallas_call(factor_kernel, out_shape=(jax.ShapeDtypeStruct((4, 4, B, B...  114 us
    pallas_call x1, Pallas kernels, finish(): pl.pallas_call(finish_kernel, out_shape=(jax.ShapeDtypeStruct((1024, 32),...  13.3 us
    unnamed x14, local copies, waits for them, and re-layouts  5.8 us

profile of v3, /device:TPU:6, one launch (start us, length us, event | category | flops | bytes accessed | tf_op | source)
XLA Modules:
  0.0 134.8 jit_solution(11501882538566212826)
XLA Ops:
  0.6 0.1 pad_add_fusion.pos
  0.7 0.0 copy-start
  0.7 1.2 copy-done
  1.9 0.0 copy-start.2
  1.9 0.7 copy-done.2
  2.6 0.0 copy-start.3
  2.6 0.7 copy-done.3
  3.3 0.0 copy-start.5
  3.3 0.7 copy-done.5
  4.0 114.1 %factor.1 = (f32[4,4,128,128]{3,2,1,0:T(8,128)S(1)}, f32[8,4,4,16,128]{4,3,2,1,0:T(8,128)S(1)}, f32[2,8,4,4,16,128]{5,4,3,2,1,0:T(8,128)S(1)}, f32[4,128,256]{2,1,0:T(8,128)S(1)}) custom-call(s32[4]{0:T(128)S(1)} %copy-done.5, s32[2,32]{1,0:T(2,128)S(1)} %copy-done.3, f32[1024,256]{1,0:T(8,128)S(1)} %copy-done, f32[8,128]{1,0:T(8,128)S(1)} %bitcast.3), custom_call_target="tpu_custom_call" | custom-call | flops 200000000 | bytes 10000000 | tf_op jit(solution)/shard_map/factor/pallas_call | solution.py:358
  118.1 0.0 copy-start.1
  118.1 1.2 copy-done.1
  119.3 0.0 copy-start.4
  119.3 0.7 copy-done.4
  120.0 0.0 copy-start.6
  120.0 0.7 copy-done.6
  120.6 13.3 %finish.1 = (f32[1024,32]{1,0:T(8,128)S(1)}, f32[1024,512]{1,0:T(8,128)}) custom-call(s32[4]{0:T(128)S(1)} %copy-done.6, s32[2,32]{1,0:T(2,128)S(1)} %copy-done.4, s32[2]{0:T(128)S(1)} %pad_add_fusion.pos, f32[1024,256]{1,0:T(8,128)S(1)} %copy-done.1, f32[4,128,256]{2,1,0:T(8,128)S(1)} %get-tuple-element.6.x_ref, f32[8,128]{1,0:T(8,128)S(1)} %bitcast.4, ...), custom_call_target="tpu_custom_call" | custom-call | flops 1000000000 | bytes 8000000 | tf_op jit(solution)/shard_map/finish/pallas_call | solution.py:447
  134.0 0.8 copy.6
Async XLA Ops:
  0.7 1.2 copy-start
  1.9 0.7 copy-start.2
  2.6 0.7 copy-start.3
  3.3 0.7 copy-start.5
  118.1 1.2 copy-start.1
  119.3 0.7 copy-start.4
  120.0 0.7 copy-start.6

commit v4 on v3

v4 whole, which is shorter than its diff:
```python
import jax
import jax.numpy as jnp
from jax import lax
from jax.experimental import pallas as pl
from jax.experimental.pallas import tpu as pltpu
from jax.sharding import PartitionSpec as P

F32 = jnp.float32
HIGHEST = lax.Precision.HIGHEST
MESH = pl.DeviceIdType.MESH
B = 128


def dot(a, b, ca, cb):
    return lax.dot_general(
        a, b, (((ca,), (cb,)), ((), ())), precision=HIGHEST, preferred_element_type=F32
    )


def split(x):
    high = x.astype(jnp.bfloat16)
    return high, (x - high.astype(F32)).astype(jnp.bfloat16)


def bdot(a, b):
    return lax.dot_general(a, b, (((1,), (0,)), ((), ())), preferred_element_type=F32)


def fetch(*pairs, sem):
    copies = [pltpu.make_async_copy(src, dst, sem.at[n]) for n, (src, dst) in enumerate(pairs)]
    for cp in copies:
        cp.start()
    return copies


def factor_block(w_ref, r_ref, out_ref, tick):
    row = lax.broadcasted_iota(jnp.int32, (16, 8, B), 0) * 8 + lax.broadcasted_iota(
        jnp.int32, (16, 8, B), 1
    )
    col = lax.broadcasted_iota(jnp.int32, (16, 8, B), 2)
    r_ref[...] = jnp.where(row == col, 1.0, 0.0).astype(F32)
    for t in range(16):
        tick(t)
        w = w_ref[t]
        v = r_ref[t]
        cols = [jnp.broadcast_to(w[:, 8 * t + k:8 * t + k + 1], (8, B)) for k in range(8)]
        a = [[None] * 8 for _ in range(8)]
        for k in range(8):
            for i in range(k, 8):
                a[i][k] = jnp.broadcast_to(cols[k][i:i + 1, :], (8, B))
        wr = [jnp.broadcast_to(w[i:i + 1, :], (8, B)) for i in range(8)]
        vr = [jnp.broadcast_to(v[i:i + 1, :], (8, B)) for i in range(8)]
        rs = [None] * 8
        l = [[None] * 8 for _ in range(8)]
        for k in range(8):
            rs[k] = lax.rsqrt(a[k][k])
            for i in range(k + 1, 8):
                l[i][k] = a[i][k] * rs[k]
            for j in range(k + 1, 8):
                for i in range(j, 8):
                    a[i][j] = a[i][j] - l[i][k] * l[j][k]
            wr[k] = wr[k] * rs[k]
            vr[k] = vr[k] * rs[k]
            for i in range(k + 1, 8):
                wr[i] = wr[i] - l[i][k] * wr[k]
                vr[i] = vr[i] - l[i][k] * vr[k]
        for k in range(8):
            out_ref[8 * t + k:8 * t + k + 1, :] = vr[k][0:1, :]
        if t < 15:
            for k in range(7, -1, -1):
                for i in range(k + 1, 8):
                    wr[k] = wr[k] - l[i][k] * wr[i]
                    vr[k] = vr[k] - l[i][k] * vr[i]
                wr[k] = wr[k] * rs[k]
                vr[k] = vr[k] * rs[k]
            for u in range(t + 1, 16):
                old = w_ref[u]
                new = old
                inv = r_ref[u]
                for k in range(8):
                    factor = jnp.broadcast_to(old[:, 8 * t + k:8 * t + k + 1], (8, B))
                    new = new - factor * wr[k]
                    inv = inv - factor * vr[k]
                w_ref[u] = new
                r_ref[u] = inv


def number(p, q):
    return p * (p + 1) // 2 + q


def home(p, q):
    return (number(p, q) - 1) * 2 % 16 + (number(p, q) - 1) // 8


def factor_kernel(
    pv_any, cm_any, con_any, fd_any, lf_any, s_any,
    l_ref, pc_ref, pr_ref, x_ref, lt, rows_hi, rows_lo, cols_hi, cols_lo, lf, st, out_sem, pv, cm, con_ref, fd_ref, sem, cand, rsb, acand, za, zb, ab, af, w_ref, r_ref,
    ss_a, rs_a, ss_z, rs_z, ss_b, rs_b, ss_g, rs_g, ss_h, ss_c, rs_c, ss_w, rs_w, ss_e, rs_e, ss_o, ss_p, rs_p, ss_t, ss_x, rs_x,
):
    f = lax.axis_index("front")
    r = lax.axis_index("row")
    c = lax.axis_index("col")
    s = r // 4
    d = r % 4

    def copy(src, dst, ssem, rsem, row, col):
        return pltpu.make_async_remote_copy(
            src_ref=src, dst_ref=dst, send_sem=ssem, recv_sem=rsem,
            device_id=(f, row, col), device_id_type=MESH,
        )

    fetches = fetch(
        (pv_any, pv), (cm_any, cm), (fd_any, fd_ref), (con_any, con_ref), sem=sem
    )
    barrier = pltpu.get_barrier_semaphore()
    for k in range(1, 8):
        pl.semaphore_signal(barrier, inc=1, device_id=(f, (r + k) % 8, c), device_id_type=MESH)
    for k in range(1, 16):
        pl.semaphore_signal(barrier, inc=1, device_id=(f, r, (c + k) % 16), device_id_type=MESH)
    out_row, out_col = c % 8, 2 * r + c // 8
    in_row, in_col = c // 2, r + 8 * (c % 2)
    stays = jnp.logical_and(out_row == r, out_col == c)

    @pl.when(jnp.logical_not(stays))
    def _():
        pl.semaphore_signal(barrier, inc=1, device_id=(f, out_row, out_col), device_id_type=MESH)
        pl.semaphore_signal(barrier, inc=1, device_id=(f, in_row, in_col), device_id_type=MESH)

    cand[:, 0:8, :] = jnp.zeros((8, 8, 256), F32)
    for cp in fetches:
        cp.wait()
    for p in range(4):
        b = pv[p] % 32
        mine = jnp.logical_and(cm[s, b] == pv[p], b % 4 == d)
        rows = con_ref[pl.ds((b // 4) * B, B), :]
        rows = jnp.where(mine, rows, 0.0)
        cand[:, 8 + p * 16:24 + p * 16, :] = rows.reshape(8, 16, 256)
        line = fd_ref[pl.ds(pv[p] // 8, 1), :]
        line = jnp.where(pv[p] % 8 == r, line, 0.0)
        cand[:, p:p + 1, 0:B] = jnp.broadcast_to(line[None], (8, 1, B))
    rsb[r] = cand[r]

    pl.semaphore_wait(barrier, jnp.where(stays, 22, 24))

    def span(p):
        return pl.ds(0, 24) if p == 0 else pl.ds(8 + 16 * p, 16)

    def rs_copy(p, k):
        to = (r + k) % 8
        return copy(cand.at[to, span(p)], rsb.at[r, span(p)], ss_a.at[p, k], rs_a.at[p, r], to, c)

    for p in range(4):
        for k in range(1, 8):
            rs_copy(p, k).start()

    lane = lax.broadcasted_iota(jnp.int32, (16, B), 1)
    sub = lax.broadcasted_iota(jnp.int32, (16, B), 0)
    on_diag = lane == sub + 16 * r

    def z_copy(k):
        to = (c + k) % 16
        return copy(acand.at[0, 0], za.at[c], ss_z.at[k], rs_z.at[c], r, to)

    def b_copy(p, q):
        return copy(acand.at[p, q], zb.at[c], ss_b.at[p, q], rs_b.at[c], r, home(p, q))

    def y_copy(k):
        return copy(ab.at[r], ab.at[r], ss_c.at[k], rs_c.at[r], (r + k) % 8, c)

    def g_copy(p, q, k):
        return copy(ab, af.at[number(p, q)], ss_g.at[k], rs_g.at[p, q], r, (c + 2 * k) % 16)

    def h_copy(p, q):
        block = af.at[number(p, q)]
        return copy(block, block, ss_h.at[p, q], rs_g.at[p, q], r, c + 1 - 2 * (c % 2))

    def forwards(p, q):
        return jnp.logical_and(c % 2 == home(p, q) % 2, c != home(p, q))

    def stage_t(p):
        for q in range(p + 1):
            @pl.when(forwards(p, q))
            def _():
                copy(ab, af.at[number(p, q)], ss_g.at[1], rs_g.at[p, q], r, c).wait_recv()
                h_copy(p, q).start()

    def stage_z(p):
        for k in range(1, 8):
            frm = (r + k) % 8
            copy(
                cand.at[frm, span(p)], rsb.at[frm, span(p)], ss_a.at[p, k], rs_a.at[p, frm], frm, c
            ).wait_recv()
        rows = [rsb[n, 8 + 16 * p:24 + 16 * p, :] for n in range(8)]
        sums = [
            (rows[4 * ch] + rows[4 * ch + 1]) + (rows[4 * ch + 2] + rows[4 * ch + 3])
            for ch in range(2)
        ]
        diag = jnp.sum(rsb[:, p:p + 1, 0:B], axis=0)
        dp = jnp.where(on_diag, jnp.broadcast_to(diag, (16, B)), 0.0)
        parts = []
        for l in range(4):
            i = l % 2
            total = jnp.where(16 * l + c == pv[p], dp, 0.0)
            for ch in range(2):
                here = cm[ch, 16 * i + c] == 16 * l + c
                total = total + jnp.where(here, sums[ch][:, i * B:(i + 1) * B], 0.0)
            pc_ref[r, p, l] = total
            parts.append(total)
        for q in range(p + 1):
            total = jnp.zeros((16, B), F32)
            for l in range(4):
                total = total + jnp.where(16 * l + c == pv[q], parts[l], 0.0)
            acand[p, q] = total
        if p == 0:
            za[c] = acand[0, 0]
            for k in range(1, 16):
                z_copy(k).start()
        else:
            for q in range(p + 1):
                @pl.when(c != home(p, q))
                def _():
                    b_copy(p, q).start()

                @pl.when(c == home(p, q))
                def _():
                    zb[c] = acand[p, q]

    def stage_m(p):
        for q in range(p + 1):
            @pl.when(c == home(p, q))
            def _():
                for k in range(1, 16):
                    frm = (c + k) % 16
                    copy(acand.at[p, q], zb.at[frm], ss_b.at[p, q], rs_b.at[frm], r, frm).wait_recv()
                ab[r] = jnp.sum(zb[...], axis=0)
                for k in range(1, 8):
                    y_copy(k).start()

    def wait_ab():
        for k in range(1, 8):
            frm = (r + k) % 8
            copy(ab.at[frm], ab.at[frm], ss_c.at[k], rs_c.at[frm], frm, c).wait_recv()

    def stage_y(p):
        if p == 0:
            for k in range(1, 16):
                frm = (c + k) % 16
                copy(acand.at[0, 0], za.at[frm], ss_z.at[k], rs_z.at[frm], r, frm).wait_recv()
            af[0, r] = jnp.sum(za[...], axis=0)
            for k in range(1, 8):
                w_copy(k).start()
        else:
            for q in range(p + 1):
                @pl.when(c == home(p, q))
                def _():
                    wait_ab()
                    for k in range(1, 8):
                        g_copy(p, q, k).start()
                    af[number(p, q)] = ab[...]
                    h_copy(p, q).start()

    def w_copy(k):
        return copy(af.at[0, r], af.at[0, r], ss_w.at[k], rs_w.at[r], (r + k) % 8, c)

    def stage_a(p):
        if p == 0:
            for k in range(1, 8):
                frm = (r + k) % 8
                copy(af.at[0, frm], af.at[0, frm], ss_w.at[k], rs_w.at[frm], frm, c).wait_recv()
        else:
            for q in range(p + 1):
                @pl.when(c % 2 != home(p, q) % 2)
                def _():
                    copy(ab, af.at[number(p, q)], ss_g.at[1], rs_g.at[p, q], r, c).wait_recv()

    def ring(step, way):
        origin = (r + (8 - step + 1 if way == 0 else step - 1)) % 8
        to = (r + (1 if way == 0 else 7)) % 8
        chunk = pc_ref.at[origin]
        return copy(chunk, chunk, ss_e.at[way, step], rs_e.at[origin], to, c)

    def ring_recv(origin):
        chunk = pc_ref.at[origin]
        copy(chunk, chunk, ss_e.at[0, 1], rs_e.at[origin], r, c).wait_recv()

    def stage_ring(step):
        if step > 1:
            ring_recv((r + 8 - step + 1) % 8)
            if step <= 4:
                ring_recv((r + step - 1) % 8)
        if step <= 4:
            ring(step, 0).start()
        if step <= 3:
            ring(step, 1).start()

    chip = c // 2
    core = c % 2

    def out_copy():
        return copy(pc_ref.at[r], pr_ref.at[out_col], ss_o.at[0], rs_p.at[out_col], out_row, out_col)

    def share_recv(n):
        copy(pc_ref.at[0], pr_ref.at[n], ss_o.at[0], rs_p.at[n], r, c).wait_recv()

    def z_ring(step, way):
        n = 2 * ((chip + (8 - step + 1 if way == 0 else step - 1)) % 8) + core
        to = (c + (2 if way == 0 else 14)) % 16
        return copy(pr_ref.at[n], pr_ref.at[n], ss_p.at[way, step], rs_p.at[n], r, to)

    def twin_copy(k):
        n = 2 * ((chip + k) % 8) + core
        return copy(pr_ref.at[n], pr_ref.at[n], ss_t.at[k], rs_p.at[n], r, c + 1 - 2 * core)

    def stage_out():
        @pl.when(stays)
        def _():
            pr_ref[c] = pc_ref[r]

        @pl.when(jnp.logical_not(stays))
        def _():
            out_copy().start()

    def stage_share(step):
        if step == 1:
            @pl.when(jnp.logical_not(stays))
            def _():
                share_recv(c)
            twin_copy(0).start()
        else:
            share_recv(2 * ((chip + 8 - step + 1) % 8) + core)
            twin_copy(8 - step + 1).start()
            if step <= 4:
                share_recv(2 * ((chip + step - 1) % 8) + core)
                twin_copy(step - 1).start()
        if step <= 4:
            z_ring(step, 0).start()
        if step <= 3:
            z_ring(step, 1).start()

    def x_copy(m):
        rows = pl.ds((2 * m + 1 - s) * B, B)
        return copy(con_ref.at[rows], x_ref.at[m], ss_x.at[m], rs_x.at[m], (r + 4) % 8, c)

    stage_z(0)
    stage_z(1)
    stage_z(2)
    stage_y(0)
    stage_z(3)
    stage_m(1)
    stage_m(2)
    stage_m(3)
    stage_out()

    actions = {
        0: [lambda: stage_y(1)],
        1: [lambda: stage_y(2)],
        2: [lambda: stage_y(3), lambda: stage_ring(1)],
        6: [lambda: x_copy(0).start()],
        8: [lambda: stage_share(1)],
        10: [lambda: stage_t(1)],
        12: [lambda: stage_ring(2)],
        13: [lambda: x_copy(1).start()],
        17: [lambda: stage_share(2), lambda: stage_t(2)],
        21: [lambda: stage_ring(3)],
        22: [lambda: x_copy(2).start()],
        23: [lambda: stage_t(3)],
        26: [lambda: stage_share(3)],
        30: [lambda: stage_ring(4)],
        31: [lambda: x_copy(3).start()],
        35: [lambda: stage_share(4)],
        39: [lambda: stage_ring(5)],
        43: [lambda: stage_share(5)],
    }

    def block(p, carry):
        for n in range(4):
            @pl.when(p == n)
            def _():
                stage_a(n)

        def left_block(q, carry):
            def minus(j, acc):
                return acc - dot(l_ref[p, j], l_ref[q, j], 1, 1)

            acc = lax.fori_loop(0, q, minus, af[number(p, q)].reshape(B, B))
            l_ref[p, q] = dot(acc, l_ref[q, q], 1, 1)
            return carry

        lax.fori_loop(0, p, left_block, 0)

        def minus(j, acc):
            low = l_ref[p, j]
            return acc - dot(low, low, 1, 1)

        acc = lax.fori_loop(0, p, minus, af[number(p, p)].reshape(B, B))
        w_ref[...] = acc.reshape(16, 8, B)

        def tick(t):
            for n in range(4):
                if 16 * n + t in actions:
                    @pl.when(p == n)
                    def _():
                        for act in actions[16 * n + t]:
                            act()

        factor_block(w_ref, r_ref, l_ref.at[p, p], tick)
        return carry

    lax.fori_loop(0, 4, block, 0)

    for k in range(8):
        share_recv(2 * k + 1 - core)
    for p in range(4):
        for k in range(8):
            lt[p, :, k * B:(k + 1) * B] = jnp.concatenate([pr_ref[2 * n + k % 2, p, k // 2] for n in range(8)], axis=0)
        for l in range(4):
            lt[p, :, 1024 + l * B:1024 + (l + 1) * B] = pc_ref[:, p, l].reshape(B, B)
    for p in range(4):
        acc = lt[p]
        if p > 0:
            low = jnp.concatenate([l_ref[p, q] for q in range(p)], axis=1)
            acc = acc - dot(low, lt[0:p].reshape(p * B, 1536), 1, 0)
        lt[p] = dot(l_ref[p, p], acc, 1, 0)
        if p >= 2:
            for k in range(8):
                gone = jnp.logical_or(8 * k + r == pv[0], 8 * k + r == pv[1])
                kept = lt[p, :, k * B:(k + 1) * B]
                lt[p, :, k * B:(k + 1) * B] = jnp.where(gone, 0.0, kept)
        hi, lo = split(lt[p])
        rows_hi[:, p * B:(p + 1) * B] = hi[:, 0:1024].T
        rows_lo[:, p * B:(p + 1) * B] = lo[:, 0:1024].T
        cols_hi[p * B:(p + 1) * B, :] = hi[:, 1024:1536]
        cols_lo[p * B:(p + 1) * B, :] = lo[:, 1024:1536]
    lf[...] = lt[c // 4, pl.ds(pl.multiple_of((c % 4) * 32, 32), 32), 0:1024]
    lf_copy = pltpu.make_async_copy(lf, lf_any, out_sem.at[2])
    lf_copy.start()
    for m in range(4):
        x_copy(m).wait()
    row = lax.broadcasted_iota(jnp.int32, (B, B), 0)
    col = lax.broadcasted_iota(jnp.int32, (B, B), 1)
    stores = []
    for half in range(2):
        part = slice(half * 512, (half + 1) * 512)
        st[part, :] = (
            bdot(rows_hi[part, :], cols_hi[...])
            + (bdot(rows_hi[part, :], cols_lo[...]) + bdot(rows_lo[part, :], cols_hi[...]))
        )
        for m in range(4):
            k = 4 * half + m
            own = con_ref[pl.ds(pl.multiple_of((2 * m + s) * B, B), B), :]
            other = x_ref[m]
            row_gone = 8 * k + r == pv[0]
            for p in range(1, 4):
                row_gone = jnp.logical_or(row_gone, 8 * k + r == pv[p])
            own_row = cm[s, 8 * m + r] == 8 * k + r
            other_row = cm[1 - s, 8 * m + r] == 8 * k + r
            dk = jnp.where(row == col, jnp.broadcast_to(fd_ref[k:k + 1, :], (B, B)), 0.0)
            for l in range(4):
                i = l % 2
                front_col = 16 * l + c
                gone = row_gone
                for p in range(4):
                    gone = jnp.logical_or(gone, front_col == pv[p])
                own_here = jnp.logical_and(own_row, cm[s, 16 * i + c] == front_col)
                other_here = jnp.logical_and(other_row, cm[1 - s, 16 * i + c] == front_col)
                tile = jnp.where(own_here, own[:, i * B:(i + 1) * B], 0.0)
                tile = tile + jnp.where(other_here, other[:, i * B:(i + 1) * B], 0.0)
                tile = tile + jnp.where(8 * k + r == front_col, dk, 0.0)
                at = (slice(k * B, (k + 1) * B), slice(l * B, (l + 1) * B))
                st[at] = jnp.where(gone, 0.0, tile - st[at])
        store = pltpu.make_async_copy(
            st.at[pl.ds(half * 512, 512)], s_any.at[pl.ds(half * 512, 512)], out_sem.at[half]
        )
        store.start()
        stores.append(store)
    for k in range(8):
        twin_copy(k).wait_send()

    @pl.when(jnp.logical_not(stays))
    def _():
        out_copy().wait_send()
    for step in range(1, 5):
        ring(step, 0).wait_send()
        z_ring(step, 0).wait_send()
        if step <= 3:
            ring(step, 1).wait_send()
            z_ring(step, 1).wait_send()
    for p in range(4):
        for k in range(1, 8):
            rs_copy(p, k).wait_send()
    for k in range(1, 8):
        w_copy(k).wait_send()
    for k in range(1, 16):
        z_copy(k).wait_send()
    for p in range(1, 4):
        for q in range(p + 1):
            @pl.when(c != home(p, q))
            def _():
                b_copy(p, q).wait_send()

            @pl.when(c == home(p, q))
            def _():
                for k in range(1, 8):
                    y_copy(k).wait_send()
                for k in range(1, 8):
                    g_copy(p, q, k).wait_send()

            @pl.when(c % 2 == home(p, q) % 2)
            def _():
                h_copy(p, q).wait_send()
    for store in stores:
        store.wait()
    lf_copy.wait()


def factor(pv, cm, contrib, fd):
    dma = pltpu.SemaphoreType.DMA
    hbm = pl.BlockSpec(memory_space=pltpu.HBM)
    return pl.pallas_call(
        factor_kernel,
        out_shape=(
            jax.ShapeDtypeStruct((32, 1024), F32),
            jax.ShapeDtypeStruct((1024, 512), F32),
        ),
        in_specs=[hbm] * 4,
        out_specs=(hbm, hbm),
        scratch_shapes=[
            pltpu.VMEM((4, 4, B, B), F32),
            pltpu.VMEM((8, 4, 4, 16, B), F32),
            pltpu.VMEM((16, 4, 4, 16, B), F32),
            pltpu.VMEM((4, B, 256), F32),
            pltpu.VMEM((4, B, 1536), F32),
            pltpu.VMEM((1024, 512), jnp.bfloat16),
            pltpu.VMEM((1024, 512), jnp.bfloat16),
            pltpu.VMEM((512, 512), jnp.bfloat16),
            pltpu.VMEM((512, 512), jnp.bfloat16),
            pltpu.VMEM((32, 1024), F32),
            pltpu.VMEM((1024, 512), F32),
            dma((3,)),
            pltpu.SMEM((4,), jnp.int32),
            pltpu.SMEM((2, 32), jnp.int32),
            pltpu.VMEM((1024, 256), F32),
            pltpu.VMEM((8, B), F32),
            dma((4,)),
            pltpu.VMEM((8, 72, 256), F32),
            pltpu.VMEM((8, 72, 256), F32),
            pltpu.VMEM((4, 4, 16, B), F32),
            pltpu.VMEM((16, 16, B), F32),
            pltpu.VMEM((16, 16, B), F32),
            pltpu.VMEM((8, 16, B), F32),
            pltpu.VMEM((10, 8, 16, B), F32),
            pltpu.VMEM((16, 8, B), F32),
            pltpu.VMEM((16, 8, B), F32),
            dma((4, 8)), dma((4, 8)), dma((16,)), dma((16,)), dma((4, 4)), dma((16,)),
            dma((16,)), dma((4, 4)), dma((4, 4)), dma((8,)), dma((8,)), dma((8,)), dma((8,)),
            dma((2, 5)), dma((8,)), dma((1,)), dma((2, 5)), dma((16,)), dma((8,)), dma((4,)), dma((4,)),
        ],
        compiler_params=pltpu.CompilerParams(
            collective_id=0, has_side_effects=True, vmem_limit_bytes=60 << 20
        ),
        name="factor",
        cost_estimate=pl.CostEstimate(flops=200_000_000, bytes_accessed=10_000_000, transcendentals=0),
    )(pv, cm, contrib, fd)


def per_device(contrib, front_diag, child_map, pivots):
    fd = front_diag.reshape(8, B)
    lf, schur = factor(pivots, child_map, contrib, fd)
    return lf.T, schur


def solution(mesh):
    placed = (P(("front", "row"), "col"), P(("front", "row")), P("front", None), P("front"))
    return jax.shard_map(
        per_device,
        mesh=mesh,
        in_specs=placed,
        out_specs=(P(("front", "row"), "col"), P(("front", "row"), "col")),
        check_vma=False,
    )
```

time: 136 us -> 106 us (0.78)
  the two profiles are of different devices: /device:TPU:6 before, /device:TPU:258 now
where the time goes in v4:
time: 106 us; the launch traced here: 105 us
  Pallas kernels  100 us (94%)
  local copies, waits for them, and re-layouts  4.65 us (4%)
    pallas_call x1, Pallas kernels, factor(): pl.pallas_call(factor_kernel, out_shape=(jax.ShapeDtypeStruct((32, 1024),...  100 us
    unnamed x2, local copies, waits for them, and re-layouts  4.65 us

profile of v4, /device:TPU:258, one launch (start us, length us, event | category | flops | bytes accessed | tf_op | source)
XLA Modules:
  0.0 105.3 jit_solution(7503793456162362605)
XLA Ops:
  0.6 100.0 %factor.1 = (f32[32,1024]{1,0:T(8,128)}, f32[1024,512]{1,0:T(8,128)}) custom-call(s32[4]{0:T(128)} %pv_any.1, s32[2,32]{1,0:T(2,128)} %cm_any.1, f32[1024,256]{1,0:T(8,128)} %con_any.1, f32[8,128]{1,0:T(8,128)} %bitcast.3), custom_call_target="tpu_custom_call" | custom-call | flops 200000000 | bytes 10000000 | tf_op jit(solution)/shard_map/factor/pallas_call | solution.py:520
  100.7 1.6 %copy.8 = f32[1024,32]{0,1:T(8,128)} copy(f32[1024,32]{0,1:T(8,128)} %bitcast.2) | data formatting | bytes 262144
  102.2 3.1 %copy.9 = f32[1024,512]{1,0:T(8,128)} copy(f32[1024,512]{1,0:T(8,128)} %get-tuple-element.9) | data formatting | bytes 4194304

commit v5 on v4

--- a/solution.py
+++ b/solution.py
@@ -94,8 +94,8 @@
 
 
 def factor_kernel(
-    pv_any, cm_any, con_any, fd_any, lf_any, s_any,
-    l_ref, pc_ref, pr_ref, x_ref, lt, rows_hi, rows_lo, cols_hi, cols_lo, lf, st, out_sem, pv, cm, con_ref, fd_ref, sem, cand, rsb, acand, za, zb, ab, af, w_ref, r_ref,
+    pv_any, cm_any, con_any, fd_any, lf, st,
+    l_ref, pc_ref, pr_ref, x_ref, lt, rows_hi, rows_lo, cols_hi, cols_lo, pv, cm, con_ref, fd_ref, sem, cand, rsb, acand, za, zb, ab, af, w_ref, r_ref,
     ss_a, rs_a, ss_z, rs_z, ss_b, rs_b, ss_g, rs_g, ss_h, ss_c, rs_c, ss_w, rs_w, ss_e, rs_e, ss_o, ss_p, rs_p, ss_t, ss_x, rs_x,
 ):
     f = lax.axis_index("front")
@@ -433,13 +433,10 @@
         cols_hi[p * B:(p + 1) * B, :] = hi[:, 1024:1536]
         cols_lo[p * B:(p + 1) * B, :] = lo[:, 1024:1536]
     lf[...] = lt[c // 4, pl.ds(pl.multiple_of((c % 4) * 32, 32), 32), 0:1024]
-    lf_copy = pltpu.make_async_copy(lf, lf_any, out_sem.at[2])
-    lf_copy.start()
     for m in range(4):
         x_copy(m).wait()
     row = lax.broadcasted_iota(jnp.int32, (B, B), 0)
     col = lax.broadcasted_iota(jnp.int32, (B, B), 1)
-    stores = []
     for half in range(2):
         part = slice(half * 512, (half + 1) * 512)
         st[part, :] = (
@@ -469,11 +466,6 @@
                 tile = tile + jnp.where(8 * k + r == front_col, dk, 0.0)
                 at = (slice(k * B, (k + 1) * B), slice(l * B, (l + 1) * B))
                 st[at] = jnp.where(gone, 0.0, tile - st[at])
-        store = pltpu.make_async_copy(
-            st.at[pl.ds(half * 512, 512)], s_any.at[pl.ds(half * 512, 512)], out_sem.at[half]
-        )
-        store.start()
-        stores.append(store)
     for k in range(8):
         twin_copy(k).wait_send()
 
@@ -509,14 +501,12 @@
             @pl.when(c % 2 == home(p, q) % 2)
             def _():
                 h_copy(p, q).wait_send()
-    for store in stores:
-        store.wait()
-    lf_copy.wait()
 
 
 def factor(pv, cm, contrib, fd):
     dma = pltpu.SemaphoreType.DMA
     hbm = pl.BlockSpec(memory_space=pltpu.HBM)
+    vm = pl.BlockSpec(memory_space=pltpu.VMEM)
     return pl.pallas_call(
         factor_kernel,
         out_shape=(
@@ -524,7 +514,7 @@
             jax.ShapeDtypeStruct((1024, 512), F32),
         ),
         in_specs=[hbm] * 4,
-        out_specs=(hbm, hbm),
+        out_specs=(vm, vm),
         scratch_shapes=[
             pltpu.VMEM((4, 4, B, B), F32),
             pltpu.VMEM((8, 4, 4, 16, B), F32),
@@ -535,9 +525,6 @@
             pltpu.VMEM((1024, 512), jnp.bfloat16),
             pltpu.VMEM((512, 512), jnp.bfloat16),
             pltpu.VMEM((512, 512), jnp.bfloat16),
-            pltpu.VMEM((32, 1024), F32),
-            pltpu.VMEM((1024, 512), F32),
-            dma((3,)),
             pltpu.SMEM((4,), jnp.int32),
             pltpu.SMEM((2, 32), jnp.int32),
             pltpu.VMEM((1024, 256), F32),

time: 106 us -> 106 us (level)
  the two profiles are of different devices: /device:TPU:258 before, /device:TPU:256 now
where the time goes in v5:
time: 106 us
  Pallas kernels  101 us (95%)
  local copies, waits for them, and re-layouts  4.65 us (4%)
    pallas_call x1, Pallas kernels, factor(): pl.pallas_call(factor_kernel, out_shape=(jax.ShapeDtypeStruct((32, 1024),...  101 us
    unnamed x2, local copies, waits for them, and re-layouts  4.65 us

profile of v5, /device:TPU:256, one launch (start us, length us, event | category | flops | bytes accessed | tf_op | source)
XLA Modules:
  0.0 106.1 jit_solution(16695326181830399005)
XLA Ops:
  0.6 100.8 %factor.1 = (f32[32,1024]{1,0:T(8,128)}, f32[1024,512]{1,0:T(8,128)}) custom-call(s32[4]{0:T(128)} %pv_any.1, s32[2,32]{1,0:T(2,128)} %cm_any.1, f32[1024,256]{1,0:T(8,128)} %con_any.1, f32[8,128]{1,0:T(8,128)} %bitcast.3), custom_call_target="tpu_custom_call" | custom-call | flops 200000000 | bytes 10000000 | tf_op jit(solution)/shard_map/factor/pallas_call | solution.py:510
  101.4 1.6 %copy.8 = f32[1024,32]{0,1:T(8,128)} copy(f32[1024,32]{0,1:T(8,128)} %bitcast.2) | data formatting | bytes 262144
  103.0 3.1 %copy.9 = f32[1024,512]{1,0:T(8,128)} copy(f32[1024,512]{1,0:T(8,128)} %get-tuple-element.9) | data formatting | bytes 4194304

commit v6 on v4

--- a/solution.py
+++ b/solution.py
@@ -356,21 +356,20 @@
         0: [lambda: stage_y(1)],
         1: [lambda: stage_y(2)],
         2: [lambda: stage_y(3), lambda: stage_ring(1)],
-        6: [lambda: x_copy(0).start()],
         8: [lambda: stage_share(1)],
+        9: [lambda: stage_ring(2)],
         10: [lambda: stage_t(1)],
-        12: [lambda: stage_ring(2)],
-        13: [lambda: x_copy(1).start()],
-        17: [lambda: stage_share(2), lambda: stage_t(2)],
-        21: [lambda: stage_ring(3)],
-        22: [lambda: x_copy(2).start()],
-        23: [lambda: stage_t(3)],
-        26: [lambda: stage_share(3)],
-        30: [lambda: stage_ring(4)],
-        31: [lambda: x_copy(3).start()],
-        35: [lambda: stage_share(4)],
-        39: [lambda: stage_ring(5)],
-        43: [lambda: stage_share(5)],
+        15: [lambda: stage_share(2)],
+        16: [lambda: stage_ring(3)],
+        17: [lambda: stage_t(2)],
+        22: [lambda: stage_share(3)],
+        23: [lambda: stage_ring(4)],
+        24: [lambda: stage_t(3)],
+        29: [lambda: stage_share(4)],
+        30: [lambda: stage_ring(5)],
+        31: [lambda: x_copy(0).start(), lambda: x_copy(1).start()],
+        36: [lambda: stage_share(5)],
+        37: [lambda: x_copy(2).start(), lambda: x_copy(3).start()],
     }
 
     def block(p, carry):

time: 106 us -> 111 us (1.047)
  the two profiles are of different devices: /device:TPU:258 before, /device:TPU:38 now
where the time goes in v6:
time: 111 us
  Pallas kernels  105 us (95%)
  local copies, waits for them, and re-layouts  4.65 us (4%)
    pallas_call x1, Pallas kernels, factor(): pl.pallas_call(factor_kernel, out_shape=(jax.ShapeDtypeStruct((32, 1024),...  105 us
    unnamed x2, local copies, waits for them, and re-layouts  4.65 us

profile of v6, /device:TPU:38, one launch (start us, length us, event | category | flops | bytes accessed | tf_op | source)
XLA Modules:
  0.0 110.8 jit_solution(5236656697870815928)
XLA Ops:
  0.6 105.5 %factor.1 = (f32[32,1024]{1,0:T(8,128)}, f32[1024,512]{1,0:T(8,128)}) custom-call(s32[4]{0:T(128)} %pv_any.1, s32[2,32]{1,0:T(2,128)} %cm_any.1, f32[1024,256]{1,0:T(8,128)} %con_any.1, f32[8,128]{1,0:T(8,128)} %bitcast.3), custom_call_target="tpu_custom_call" | custom-call | flops 200000000 | bytes 10000000 | tf_op jit(solution)/shard_map/factor/pallas_call | solution.py:519
  106.1 1.6 %copy.8 = f32[1024,32]{0,1:T(8,128)} copy(f32[1024,32]{0,1:T(8,128)} %bitcast.2) | data formatting | bytes 262144
  107.7 3.1 %copy.9 = f32[1024,512]{1,0:T(8,128)} copy(f32[1024,512]{1,0:T(8,128)} %get-tuple-element.9) | data formatting | bytes 4194304

commit v7 on v4

--- a/solution.py
+++ b/solution.py
@@ -347,27 +347,27 @@
     stage_z(2)
     stage_y(0)
     stage_z(3)
+    stage_out()
+    x_copy(0).start()
     stage_m(1)
     stage_m(2)
     stage_m(3)
-    stage_out()
 
     actions = {
         0: [lambda: stage_y(1)],
         1: [lambda: stage_y(2)],
         2: [lambda: stage_y(3), lambda: stage_ring(1)],
-        6: [lambda: x_copy(0).start()],
+        6: [lambda: x_copy(1).start()],
         8: [lambda: stage_share(1)],
         10: [lambda: stage_t(1)],
         12: [lambda: stage_ring(2)],
-        13: [lambda: x_copy(1).start()],
+        13: [lambda: x_copy(2).start()],
         17: [lambda: stage_share(2), lambda: stage_t(2)],
         21: [lambda: stage_ring(3)],
-        22: [lambda: x_copy(2).start()],
+        19: [lambda: x_copy(3).start()],
         23: [lambda: stage_t(3)],
         26: [lambda: stage_share(3)],
         30: [lambda: stage_ring(4)],
-        31: [lambda: x_copy(3).start()],
         35: [lambda: stage_share(4)],
         39: [lambda: stage_ring(5)],
         43: [lambda: stage_share(5)],

time: 106 us -> 113 us (1.066)
  the two profiles are of different devices: /device:TPU:258 before, /device:TPU:6 now
where the time goes in v7:
time: 113 us
  Pallas kernels  108 us (96%)
  local copies, waits for them, and re-layouts  4.65 us (4%)
    pallas_call x1, Pallas kernels, factor(): pl.pallas_call(factor_kernel, out_shape=(jax.ShapeDtypeStruct((32, 1024),...  108 us
    unnamed x2, local copies, waits for them, and re-layouts  4.65 us

profile of v7, /device:TPU:6, one launch (start us, length us, event | category | flops | bytes accessed | tf_op | source)
XLA Modules:
  0.0 113.1 jit_solution(10039154943106293906)
XLA Ops:
  0.6 107.8 %factor.1 = (f32[32,1024]{1,0:T(8,128)}, f32[1024,512]{1,0:T(8,128)}) custom-call(s32[4]{0:T(128)} %pv_any.1, s32[2,32]{1,0:T(2,128)} %cm_any.1, f32[1024,256]{1,0:T(8,128)} %con_any.1, f32[8,128]{1,0:T(8,128)} %bitcast.3), custom_call_target="tpu_custom_call" | custom-call | flops 200000000 | bytes 10000000 | tf_op jit(solution)/shard_map/factor/pallas_call | solution.py:520
  108.5 1.6 %copy.8 = f32[1024,32]{0,1:T(8,128)} copy(f32[1024,32]{0,1:T(8,128)} %bitcast.2) | data formatting | bytes 262144
  110.0 3.1 %copy.9 = f32[1024,512]{1,0:T(8,128)} copy(f32[1024,512]{1,0:T(8,128)} %get-tuple-element.9) | data formatting | bytes 4194304

commit v8 on v4

--- a/solution.py
+++ b/solution.py
@@ -379,22 +379,22 @@
             def _():
                 stage_a(n)
 
-        def left_block(q, carry):
-            def minus(j, acc):
-                return acc - dot(l_ref[p, j], l_ref[q, j], 1, 1)
-
-            acc = lax.fori_loop(0, q, minus, af[number(p, q)].reshape(B, B))
-            l_ref[p, q] = dot(acc, l_ref[q, q], 1, 1)
-            return carry
-
-        lax.fori_loop(0, p, left_block, 0)
-
-        def minus(j, acc):
-            low = l_ref[p, j]
-            return acc - dot(low, low, 1, 1)
-
-        acc = lax.fori_loop(0, p, minus, af[number(p, p)].reshape(B, B))
-        w_ref[...] = acc.reshape(16, 8, B)
+        def beside(n, count):
+            return jnp.concatenate([l_ref[n, j] for j in range(count)], axis=1)
+
+        for n in range(4):
+            @pl.when(p == n)
+            def _():
+                for q in range(n):
+                    acc = af[number(n, q)].reshape(B, B)
+                    if q > 0:
+                        acc = acc - dot(beside(n, q), beside(q, q), 1, 1)
+                    l_ref[n, q] = dot(acc, l_ref[q, q], 1, 1)
+                acc = af[number(n, n)].reshape(B, B)
+                if n > 0:
+                    low = beside(n, n)
+                    acc = acc - dot(low, low, 1, 1)
+                w_ref[...] = acc.reshape(16, 8, B)
 
         def tick(t):
             for n in range(4):

time: 106 us -> 105 us (level)
  the two profiles are of different devices: /device:TPU:258 before, /device:TPU:262 now
where the time goes in v8:
time: 105 us
  Pallas kernels  99.3 us (95%)
  local copies, waits for them, and re-layouts  4.65 us (4%)
    pallas_call x1, Pallas kernels, factor(): pl.pallas_call(factor_kernel, out_shape=(jax.ShapeDtypeStruct((32, 1024),...  99.3 us
    unnamed x2, local copies, waits for them, and re-layouts  4.65 us

profile of v8, /device:TPU:262, one launch (start us, length us, event | category | flops | bytes accessed | tf_op | source)
XLA Modules:
  0.0 104.6 jit_solution(2137541706097751752)
XLA Ops:
  0.6 99.3 %factor.1 = (f32[32,1024]{1,0:T(8,128)}, f32[1024,512]{1,0:T(8,128)}) custom-call(s32[4]{0:T(128)} %pv_any.1, s32[2,32]{1,0:T(2,128)} %cm_any.1, f32[1024,256]{1,0:T(8,128)} %con_any.1, f32[8,128]{1,0:T(8,128)} %bitcast.3), custom_call_target="tpu_custom_call" | custom-call | flops 200000000 | bytes 10000000 | tf_op jit(solution)/shard_map/factor/pallas_call | solution.py:520
  99.9 1.6 %copy.8 = f32[1024,32]{0,1:T(8,128)} copy(f32[1024,32]{0,1:T(8,128)} %bitcast.2) | data formatting | bytes 262144
  101.5 3.1 %copy.9 = f32[1024,512]{1,0:T(8,128)} copy(f32[1024,512]{1,0:T(8,128)} %get-tuple-element.9) | data formatting | bytes 4194304
